TPU v7x, 256 devices: a whole 4x4x8 slice. The times are simulated.
256 devices in a mesh: expert: 2 (over z_lo), batch: 4 (over x), seq: 32 (over y, z_hi, core).
Axes of the slice: x: 4, y: 4, z: 8 (z_hi: 4, z_lo: 2; z = z_hi * 2 + z_lo), core: 2. Of those that a mesh axis runs over, the one named last changes fastest.
Arguments:
- queries: bfloat16 [2, 4, 2, 3072, 4096], P('expert', 'batch', None, 'seq'), may hold values from -36 to 36
- keys: bfloat16 [2, 4, 2, 3072, 4096], P('expert', 'batch', None, 'seq'), may hold values from -21 to 21
- values: bfloat16 [2, 4, 2, 3072, 4096], P('expert', 'batch', None, 'seq'), may hold values from -6 to 6
- latents: bfloat16 [2, 4, 3072, 4096], P('expert', 'batch', 'seq'), may hold values from -6 to 6
- gain: bfloat16 [2, 4096], P('expert'), may hold values from 0.099609375 to 1.8984375
- steps_table: int32 [2, 4], P('expert', 'batch'), may hold values from 0 to 38
- flags: int32 [4], P('batch'), may hold values 0 or 1
Outputs:
- denoised: bfloat16 [2, 4, 3072, 4096], P('expert', 'batch', 'seq')
- next_latents: bfloat16 [2, 4, 3072, 4096], P('expert', 'batch', 'seq')
All inputs are finite; a program needn't handle non-finite values. No bound on the sum of `flags` on one device may be relied on, other than what follows from the above.
Results may differ from a plain program's by a relative error of at most 0.006.
Values may be sent and summed in bfloat16 or wider, within the bound.
No kernel may reach another device: no remote copies, remote signals or barrier semaphores. Data moves between devices by JAX's collectives and lax.ppermute only.
A program may use at most 64 MiB of HBM per device.

v0:
```python
import functools
import math

import jax
import jax.numpy as jnp
from jax import lax
from jax.experimental import pallas as pl
from jax.experimental.pallas import tpu as pltpu
from jax.sharding import Mesh
from jax.sharding import PartitionSpec as P

HDIM = 128
STEPS = 40
GUIDANCE = 3.5
FLOW_SHIFT = 5.0
BF16 = jnp.bfloat16
F32 = jnp.float32

Y, Z, CORE = SEQ = ("seq_y", "seq_z", "seq_core")
FAR = 4
NEAR = 8
LOG2_SCALE = math.log2(math.e) / math.sqrt(HDIM)
SAFE_LOG2 = 100.0
CONTRACT_LAST = (((1,), (1,)), ((), ()))
VMEM_LIMIT = 32 << 20
ATTEND_VMEM = 52 << 20


def in_vmem(a):
    return pltpu.with_memory_space_constraint(a, pltpu.VMEM)


def sigma_of(step):
    level = 1.0 - step.astype(F32) / STEPS
    return FLOW_SHIFT * level / (1.0 + (FLOW_SHIFT - 1.0) * level)


def pack_kernel(*refs, spans):
    count = len(spans)
    sources, out, (ins, outs, in_sems, out_sems) = refs[:count], refs[count], refs[count + 1 :]
    heads = out.shape[0]
    pieces, at = [], 0
    for source, (first, rows) in zip(sources, spans):
        for branch in range(2):
            pieces.append((source.at[0, 0, branch, pl.ds(first, rows)], at, rows))
            at += rows
    reads = [
        pltpu.make_async_copy(source, ins.at[pl.ds(at, rows)], in_sems.at[n])
        for n, (source, at, rows) in enumerate(pieces)
    ]
    writes = [
        pltpu.make_async_copy(outs.at[:, pl.ds(at, rows)], out.at[:, pl.ds(at, rows)], out_sems.at[n])
        for n, (_, at, rows) in enumerate(pieces)
    ]
    for read in reads:
        read.start()
    for (_, at, rows), read, write in zip(pieces, reads, writes):
        read.wait()
        for h in range(heads):
            outs[h, at : at + rows] = ins[at : at + rows, h * HDIM : (h + 1) * HDIM]
        write.start()
    for write in writes:
        write.wait()


def pack(sources, spans):
    width = sources[0].shape[-1]
    heads = width // HDIM
    total = sum(2 * rows for _, rows in spans)
    count = 2 * len(spans)
    return pl.pallas_call(
        functools.partial(pack_kernel, spans=spans),
        in_specs=[pl.BlockSpec(memory_space=pltpu.HBM) for _ in sources],
        out_specs=pl.BlockSpec(memory_space=pltpu.HBM),
        out_shape=pltpu.HBM((heads, total, HDIM), BF16),
        scratch_shapes=[
            pltpu.VMEM((total, width), BF16),
            pltpu.VMEM((heads, total, HDIM), BF16),
            pltpu.SemaphoreType.DMA((count,)),
            pltpu.SemaphoreType.DMA((count,)),
        ],
        compiler_params=pltpu.CompilerParams(vmem_limit_bytes=VMEM_LIMIT),
    )(*(pltpu.with_memory_space_constraint(a, pltpu.HBM) for a in sources))


def attend_kernel(place, *refs, arrays, shard, part, first, groups, normed):
    kv_ref, q_ref = refs[0], refs[arrays - 1]
    norms_in = refs[arrays] if normed else None
    *outs, norms = refs[-FAR - 1 :]
    peers = kv_ref.shape[0]
    rows = groups * NEAR * part

    def resident(n, at=slice(None)):
        return kv_ref[at, n * shard : (n + 1) * shard].reshape(-1, HDIM)

    def most(vectors):
        squares = jnp.dot(vectors * vectors, jnp.ones((HDIM, HDIM), BF16), preferred_element_type=F32)
        return jnp.max(squares) * 1.01

    @pl.when(pl.program_id(0) == 0)
    def _():
        for c in range(2):
            norms[c] = norms_in[c] if normed else most(resident(c))

    queries, bound = [], 0.0
    for c in range(2):
        own = slice(first + c * part, first + (c + 1) * part)
        pieces = []
        for g in range(groups):
            other = (pl.program_id(0) * groups + g) ^ place[0]
            for y in range(NEAR // 2):
                pieces.append(q_ref[pl.ds(y * 2 * FAR + other * 2, 2), own])
        q = jnp.concatenate(pieces, axis=0).reshape(rows, HDIM)
        queries.append(q)
        bound = jnp.maximum(bound, most(q) * norms[c])
    unshifted = bound <= (SAFE_LOG2 / LOG2_SCALE) ** 2

    def scores(c, k):
        return lax.dot_general(queries[c], k, CONTRACT_LAST, preferred_element_type=F32) * LOG2_SCALE

    def lanes(weights):
        return sum(weights[:, at : at + HDIM] for at in range(0, weights.shape[1], HDIM))

    def weigh(weights, v):
        return jnp.dot(weights.astype(BF16), v, preferred_element_type=F32)

    def finish(sums, totals):
        cond, uncond = (s / jnp.sum(t, axis=1, keepdims=True) for s, t in zip(sums, totals))
        guided = (uncond + GUIDANCE * (cond - uncond)).astype(BF16).reshape(groups, NEAR, part, HDIM)
        for step in range(FAR // groups):

            @pl.when(pl.program_id(0) == step)
            def _():
                for g in range(groups):
                    outs[step * groups + g][...] = guided[g]

    @pl.when(unshifted)
    def _():
        ahead = [scores(c, resident(c)) for c in range(2)]
        weights = [jnp.exp2(a) for a in ahead]
        finish([weigh(w, resident(2 + c)) for c, w in enumerate(weights)], [lanes(w) for w in weights])

    @pl.when(jnp.logical_not(unshifted))
    def _():
        sums, totals = [], []
        per = 4
        for c in range(2):

            def highest(j, m):
                return jnp.maximum(m, jnp.max(scores(c, resident(c, pl.ds(j * per, per))), axis=1, keepdims=True))

            top = lax.fori_loop(0, peers // per, highest, jnp.full((rows, 1), -jnp.inf, F32))

            def add(j, carry):
                at = pl.ds(j * per, per)
                weights = jnp.exp2(scores(c, resident(c, at)) - top)
                return carry[0] + weigh(weights, resident(2 + c, at)), carry[1] + lanes(weights)

            zero = jnp.zeros((rows, HDIM), F32)
            total, count = lax.fori_loop(0, peers // per, add, (zero, zero))
            sums.append(total)
            totals.append(count)
        finish(sums, totals)


def attend(place, arrays, shard, part, first, groups, norms=()):
    smem = pl.BlockSpec(memory_space=pltpu.SMEM)
    whole = pl.BlockSpec(memory_space=pltpu.VMEM)
    *outs, norms = pl.pallas_call(
        functools.partial(
            attend_kernel,
            arrays=len(arrays),
            shard=shard,
            part=part,
            first=first,
            groups=groups,
            normed=bool(norms),
        ),
        grid=(FAR // groups,),
        in_specs=[smem] + [whole for _ in arrays] + [smem for _ in norms],
        out_specs=[whole] * FAR + [smem],
        out_shape=[jax.ShapeDtypeStruct((NEAR, part, HDIM), BF16)] * FAR + [jax.ShapeDtypeStruct((2,), F32)],
        compiler_params=pltpu.CompilerParams(vmem_limit_bytes=ATTEND_VMEM),
    )(place, *(in_vmem(a) for a in arrays), *norms)
    return outs, norms


def regroup_kernel(*refs):
    *sources, out = refs
    for d, source in enumerate(sources):
        out[:, d] = source[...]


def regroup(pieces):
    near, part, _ = pieces[0].shape
    return pl.pallas_call(
        regroup_kernel,
        in_specs=[pl.BlockSpec(memory_space=pltpu.VMEM)] * len(pieces),
        out_specs=pl.BlockSpec(memory_space=pltpu.VMEM),
        out_shape=jax.ShapeDtypeStruct((near, len(pieces), part, HDIM), BF16),
        compiler_params=pltpu.CompilerParams(vmem_limit_bytes=VMEM_LIMIT),
    )(*(in_vmem(p) for p in pieces))


def changed_rows(place, guided, latents, gain, change, out, first):
    near, far, rows, _ = guided.shape
    heads = near * far

    def head(h):
        y, rest = divmod(h, 2 * far)
        z, core = divmod(rest, 2)
        return guided[2 * y + core, z ^ place[0]].astype(F32)

    total = None
    for h in range(heads):
        g = head(h)
        total = g * g if total is None else total + g * g
    mean = jnp.sum(total, axis=1, keepdims=True) / (heads * HDIM)
    scale = lax.rsqrt(mean + 1e-06)
    for h in range(heads):
        columns = slice(h * HDIM, (h + 1) * HDIM)
        velocity = head(h) * scale * gain[:, columns].astype(F32)
        current = latents[0, 0, first : first + rows, columns].astype(F32)
        out[:, columns] = (current + change * velocity).astype(BF16)


def move_kernel(place, steps, guided, latents, gain, out, *, first):
    change = sigma_of(steps[0, 0] + 1) - sigma_of(steps[0, 0])
    changed_rows(place, guided, latents, gain, change, out, first)


def denoise_kernel(place, steps, *refs):
    *parts, latents, gain, out = refs
    first = 0
    for guided in parts:
        rows = guided.shape[2]
        to = out.at[0, 0, pl.ds(first, rows)]
        changed_rows(place, guided, latents, gain, -sigma_of(steps[0, 0]), to, first)
        first += rows


def update(kernel, out_shape, place, steps_table, parts, latents, gain):
    smem = pl.BlockSpec(memory_space=pltpu.SMEM)
    whole = pl.BlockSpec(memory_space=pltpu.VMEM)
    return pl.pallas_call(
        kernel,
        in_specs=[smem, smem] + [whole] * (len(parts) + 2),
        out_specs=whole,
        out_shape=jax.ShapeDtypeStruct(out_shape, BF16),
        compiler_params=pltpu.CompilerParams(vmem_limit_bytes=VMEM_LIMIT),
    )(place, steps_table, *(in_vmem(a) for a in (*parts, latents, gain)))


def choose_kernel(flags, *refs):
    *pairs, out = refs
    count = len(pairs) // 2
    first = 0
    for partner, moved in zip(pairs[:count], pairs[count:]):
        rows = moved.shape[0]
        out[0, 0, first : first + rows] = jnp.where(flags[0] == 1, partner[...], moved[...])
        first += rows


def choose(flags, partner, moved, shape):
    whole = pl.BlockSpec(memory_space=pltpu.VMEM)
    operands = [*partner, *moved]
    return pl.pallas_call(
        choose_kernel,
        in_specs=[pl.BlockSpec(memory_space=pltpu.SMEM)] + [whole] * len(operands),
        out_specs=whole,
        out_shape=jax.ShapeDtypeStruct(shape, BF16),
        compiler_params=pltpu.CompilerParams(vmem_limit_bytes=VMEM_LIMIT),
    )(flags, *(in_vmem(a) for a in operands))


def per_device(queries, keys, values, latents, gain, steps_table, flags):
    tokens, width = queries.shape[3:]
    tail = tokens // 3
    head = tokens - tail
    place = lax.axis_index(Z).reshape(1).astype(jnp.int32)
    exchange = lambda a, axes: lax.all_to_all(a, axes, split_axis=0, concat_axis=0, tiled=True)
    together = lax.optimization_barrier

    def along_z(pieces):
        return [lax.ppermute(p, Z, [(i, i ^ d) for i in range(FAR)]) if d else p for d, p in enumerate(pieces)]

    kvq = exchange(pack((keys, values, queries), ((0, tokens), (0, tokens), (0, head))), SEQ)
    rest, _ = together((pack((queries,), ((head, tail),)), kvq))
    rest = exchange(rest, SEQ)
    own, norms = attend(place, (kvq,), tokens, head, 4 * tokens, groups=2)
    own, rest = together((own, rest))
    near = along_z(own)
    own, _ = attend(place, (kvq, rest), tokens, tail, 0, groups=4, norms=(norms,))
    near, own = together((near, own))
    far = along_z(own)
    guided_head = exchange(regroup(near), (Y, CORE))
    far, guided_head = together((far, guided_head))
    guided_tail = exchange(regroup(far), (Y, CORE))

    swap = lambda a: lax.ppermute(a, "expert", [(0, 1), (1, 0)])
    moved, partner = [], []
    for first, guided in ((0, guided_head), (head, guided_tail)):
        shape = (guided.shape[2], width)
        kernel = functools.partial(move_kernel, first=first)
        moved.append(update(kernel, shape, place, steps_table, (guided,), latents, gain))
        partner.append(swap(moved[-1]))
    parts = (guided_head, guided_tail)
    denoised = update(denoise_kernel, latents.shape, place, steps_table, parts, latents, gain)
    return (denoised, choose(flags, partner, moved, latents.shape))


def solution(mesh):
    sizes = (mesh.shape["expert"], mesh.shape["batch"], NEAR // 2, FAR, 2)
    torus = Mesh(mesh.devices.reshape(sizes), ("expert", "batch", *SEQ))
    placed = (
        P("expert", "batch", None, SEQ, None),
        P("expert", "batch", None, SEQ, None),
        P("expert", "batch", None, SEQ, None),
        P("expert", "batch", SEQ, None),
        P("expert", None),
        P("expert", "batch"),
        P("batch"),
    )
    return jax.shard_map(
        per_device,
        mesh=torus,
        in_specs=placed,
        out_specs=(P("expert", "batch", SEQ, None), P("expert", "batch", SEQ, None)),
        check_vma=False,
    )
```

profile of v0, /device:TPU:1, one launch (start us, length us, event | category | flops | bytes accessed | tf_op | source)
XLA Modules:
  0.0 219.3 jit_solution(12671156404451525017)
XLA Ops:
  0.6 3.4 %shard_map.86 = bf16[32,512,128]{2,1,0:T(8,128)(2,1)} custom-call(bf16[1,1,2,96,4096]{4,3,2,1,0:T(8,128)(2,1)} %refs_0_.2, bf16[1,1,2,96,4096]{4,3,2,1,0:T(8,128)(2,1)} %refs_1_.1, bf16[1,1,2,96,4096]{4,3,2,1,0:T(8,128)(2,1)} %refs_0_.3), custom_call_target="tpu_custom_call" | custom-call | tf_op jit(solution)/shard_map/pallas_call | solution.py:71
  4.1 12.8 %all-to-all-start = ((bf16[32,512,128]{2,1,0:T(8,128)(2,1)}), bf16[32,512,128]{2,1,0:T(8,128)(2,1)}, u32[]{:S(2)}, u32[]{:S(2)}) async-start(bf16[32,512,128]{2,1,0:T(8,128)(2,1)} %shard_map.86), calls=%async_computation | async-start | bytes 8388608 | tf_op jit(solution)/shard_map/all_to_all | solution.py:281
  16.9 1.8 shard_map.88
  18.7 91.4 %all-to-all-done.refs_0_ = bf16[32,512,128]{2,1,0:T(8,128)(2,1)} async-done(((bf16[32,512,128]{2,1,0:T(8,128)(2,1)}), bf16[32,512,128]{2,1,0:T(8,128)(2,1)}, u32[]{:S(2)}, u32[]{:S(2)}) %all-to-all-start) | async-done | bytes 4194336 | tf_op jit(solution)/shard_map/all_to_all | solution.py:281
  110.1 7.5 %all-to-all-start.1 = ((bf16[32,64,128]{2,1,0:T(8,128)(2,1)}), bf16[32,64,128]{2,1,0:T(8,128)(2,1)S(1)}, u32[]{:S(2)}, u32[]{:S(2)}) async-start(bf16[32,64,128]{2,1,0:T(8,128)(2,1)} %shard_map.88), calls=%async_computation.1 | async-start | bytes 1048576 | tf_op jit(solution)/shard_map/all_to_all | solution.py:281
  117.6 30.9 %shard_map.87 = (bf16[8,64,128]{2,1,0:T(8,128)(2,1)}, bf16[8,64,128]{2,1,0:T(8,128)(2,1)}, bf16[8,64,128]{2,1,0:T(8,128)(2,1)}, bf16[8,64,128]{2,1,0:T(8,128)(2,1)}, f32[2]{0:T(128)}) custom-call(s32[1]{0:T(128)} %bitcast.place, bf16[32,512,128]{2,1,0:T(8,128)(2,1)} %all-to-all-done.refs_0_), custom_call_target="tpu_custom_call" | custom-call | tf_op jit(solution)/shard_map/pallas_call | solution.py:169
  148.5 0.0 all-to-all-done.1.refs_1_
  148.5 2.6 %collective-permute-start = (bf16[8,64,128]{2,1,0:T(8,128)(2,1)}, bf16[8,64,128]{2,1,0:T(8,128)(2,1)S(1)}, u32[]{:S(2)}, u32[]{:S(2)}) collective-permute-start(bf16[8,64,128]{2,1,0:T(8,128)(2,1)} %get-tuple-element.36), channel_id=1, source_target_pairs={{0,2},{2,0},{4,6},{6,4},{1,3},{3,1},{5,7},{7,5},{8,10},{10,8},{12,... | collective-permute-start | bytes 393224 | tf_op jit(solution)/shard_map/ppermute | solution.py:285
  151.1 3.3 %collective-permute-start.1 = (bf16[8,64,128]{2,1,0:T(8,128)(2,1)}, bf16[8,64,128]{2,1,0:T(8,128)(2,1)S(1)}, u32[]{:S(2)}, u32[]{:S(2)}) collective-permute-start(bf16[8,64,128]{2,1,0:T(8,128)(2,1)} %get-tuple-element.37), channel_id=1, source_target_pairs={{0,4},{2,6},{4,0},{6,2},{1,5},{3,7},{5,1},{7,3},{8,12},{10,14},{12... | collective-permute-start | bytes 393224 | tf_op jit(solution)/shard_map/ppermute | solution.py:285
  154.4 0.1 collective-permute-start.2
  154.5 0.0 copy-start.2
  154.5 22.9 %shard_map.89 = (bf16[8,32,128]{2,1,0:T(8,128)(2,1)}, bf16[8,32,128]{2,1,0:T(8,128)(2,1)}, bf16[8,32,128]{2,1,0:T(8,128)(2,1)}, bf16[8,32,128]{2,1,0:T(8,128)(2,1)}, f32[2]{0:T(128)}) custom-call(s32[1]{0:T(128)} %bitcast.place, bf16[32,512,128]{2,1,0:T(8,128)(2,1)} %all-to-all-done.refs_0_, bf16[32,64,128]{2,1,0:T(8,128)(2,1)S(1)} %all-to-all-done.1.refs_1_, ...), custom_call_target="tpu_custom_call" | custom-call | tf_op jit(solution)/shard_map/pallas_call | solution.py:169
  177.4 0.0 copy-start.6
  177.4 0.0 copy-start.5
  177.5 0.0 copy-start.4
  177.5 0.0 copy-start
  177.5 0.0 copy-start.1
  177.5 0.0 collective-permute-done.refs_1_
  177.5 0.0 collective-permute-done.1.refs_2_
  177.5 0.0 collective-permute-done.2.refs_3_
  177.5 0.0 copy-done.2
  177.5 0.8 shard_map.90
  178.4 0.0 copy-start.3
  178.4 5.7 %all-to-all-start.2 = ((bf16[8,4,64,128]{3,2,1,0:T(8,128)(2,1)}), bf16[8,4,64,128]{3,2,1,0:T(8,128)(2,1)S(1)}, u32[]{:S(2)}, u32[]{:S(2)}) async-start(bf16[8,4,64,128]{3,2,1,0:T(8,128)(2,1)} %shard_map.90), calls=%async_computation.2 | async-start | bytes 1048576 | tf_op jit(solution)/shard_map/all_to_all | solution.py:281
  184.1 0.0 copy-done.6
  184.1 2.1 collective-permute-start.3
  186.2 0.0 copy-done.5
  186.2 3.3 %collective-permute-start.4 = (bf16[8,32,128]{2,1,0:T(8,128)(2,1)S(1)}, bf16[8,32,128]{2,1,0:T(8,128)(2,1)S(1)}, u32[]{:S(2)}, u32[]{:S(2)}) collective-permute-start(bf16[8,32,128]{2,1,0:T(8,128)(2,1)S(1)} %copy-done.5), channel_id=1, source_target_pairs={{0,4},{2,6},{4,0},{6,2},{1,5},{3,7},{5,1},{7,3},{8,12},{10,14},{12... | collective-permute-start | bytes 196616 | tf_op jit(solution)/shard_map/ppermute | solution.py:285
  189.5 0.0 copy-done.4
  189.5 0.3 collective-permute-start.5
  190.5 0.0 collective-permute-done.3.refs_1_
  190.5 3.0 %collective-permute-done.4.refs_2_ = bf16[8,32,128]{2,1,0:T(8,128)(2,1)S(1)} collective-permute-done((bf16[8,32,128]{2,1,0:T(8,128)(2,1)S(1)}, bf16[8,32,128]{2,1,0:T(8,128)(2,1)S(1)}, u32[]{:S(2)}, u32[]{:S(2)}) %collective-permute-start.4) | collective-permute-done | bytes 65568 | tf_op jit(solution)/shard_map/ppermute | solution.py:285
  193.4 3.1 %collective-permute-done.5.refs_3_ = bf16[8,32,128]{2,1,0:T(8,128)(2,1)S(1)} collective-permute-done((bf16[8,32,128]{2,1,0:T(8,128)(2,1)S(1)}, bf16[8,32,128]{2,1,0:T(8,128)(2,1)S(1)}, u32[]{:S(2)}, u32[]{:S(2)}) %collective-permute-start.5) | collective-permute-done | bytes 65568 | tf_op jit(solution)/shard_map/ppermute | solution.py:285
  196.5 0.0 all-to-all-done.2.refs_0_.guided
  196.5 0.0 copy-done
  196.5 0.0 copy-done.1
  196.6 0.4 shard_map.93.refs_2_
  196.9 2.8 %collective-permute-start.6 = (bf16[64,4096]{1,0:T(8,128)(2,1)S(1)}, bf16[64,4096]{1,0:T(8,128)(2,1)S(1)}, u32[]{:S(2)}, u32[]{:S(2)}) collective-permute-start(bf16[64,4096]{1,0:T(8,128)(2,1)S(1)} %shard_map.93.refs_2_), channel_id=1, source_target_pairs={{0,128},{128,0},{1,129},{129,1},{2,130},{130,2},{3,131},{131,3},{4... | collective-permute-start | bytes 1572872 | tf_op jit(solution)/shard_map/ppermute | solution.py:300
  199.7 0.0 copy-done.3
  199.7 11.6 %all_to_all.20.refs_1_.guided = bf16[8,4,32,128]{3,2,1,0:T(8,128)(2,1)S(1)} all-to-all(bf16[8,4,32,128]{3,2,1,0:T(8,128)(2,1)S(1)} %shard_map.91), channel_id=1, replica_groups=mesh['expert'=2,'batch'=4,'seq_y'=4,'seq_z'=4,'seq_core'=2] {'seq_y','se..., dimensions={0} | all-to-all | bytes 524288 | tf_op jit(solution)/shard_map/all_to_all | solution.py:281
  211.3 0.2 shard_map.94.refs_3_
  211.5 0.1 collective-permute-start.7
  212.3 1.4 shard_map.92
  213.7 4.7 %collective-permute-done.7.refs_1_ = bf16[32,4096]{1,0:T(8,128)(2,1)S(1)} collective-permute-done((bf16[32,4096]{1,0:T(8,128)(2,1)S(1)}, bf16[32,4096]{1,0:T(8,128)(2,1)S(1)}, u32[]{:S(2)}, u32[]{:S(2)}) %collective-permute-start.7) | collective-permute-done | bytes 262176 | tf_op jit(solution)/shard_map/ppermute | solution.py:300
  218.4 0.0 collective-permute-done.6.refs_0_
  218.4 1.0 shard_map.95
  (1 shorter events, 0.0 us)
Async XLA Ops:
  4.1 106.0 %all-to-all-start = ((bf16[32,512,128]{2,1,0:T(8,128)(2,1)}), bf16[32,512,128]{2,1,0:T(8,128)(2,1)}, u32[]{:S(2)}, u32[]{:S(2)}) async-start(bf16[32,512,128]{2,1,0:T(8,128)(2,1)} %shard_map.86), calls=%async_computation | async-start | bytes 8388608 | tf_op jit(solution)/shard_map/all_to_all | solution.py:281
  110.1 38.4 %all-to-all-start.1 = ((bf16[32,64,128]{2,1,0:T(8,128)(2,1)}), bf16[32,64,128]{2,1,0:T(8,128)(2,1)S(1)}, u32[]{:S(2)}, u32[]{:S(2)}) async-start(bf16[32,64,128]{2,1,0:T(8,128)(2,1)} %shard_map.88), calls=%async_computation.1 | async-start | bytes 1048576 | tf_op jit(solution)/shard_map/all_to_all | solution.py:281
  148.5 28.9 %collective-permute-start = (bf16[8,64,128]{2,1,0:T(8,128)(2,1)}, bf16[8,64,128]{2,1,0:T(8,128)(2,1)S(1)}, u32[]{:S(2)}, u32[]{:S(2)}) collective-permute-start(bf16[8,64,128]{2,1,0:T(8,128)(2,1)} %get-tuple-element.36), channel_id=1, source_target_pairs={{0,2},{2,0},{4,6},{6,4},{1,3},{3,1},{5,7},{7,5},{8,10},{10,8},{12,... | collective-permute-start | bytes 393224 | tf_op jit(solution)/shard_map/ppermute | solution.py:285
  151.1 26.4 %collective-permute-start.1 = (bf16[8,64,128]{2,1,0:T(8,128)(2,1)}, bf16[8,64,128]{2,1,0:T(8,128)(2,1)S(1)}, u32[]{:S(2)}, u32[]{:S(2)}) collective-permute-start(bf16[8,64,128]{2,1,0:T(8,128)(2,1)} %get-tuple-element.37), channel_id=1, source_target_pairs={{0,4},{2,6},{4,0},{6,2},{1,5},{3,7},{5,1},{7,3},{8,12},{10,14},{12... | collective-permute-start | bytes 393224 | tf_op jit(solution)/shard_map/ppermute | solution.py:285
  154.4 23.1 %collective-permute-start.2 = (bf16[8,64,128]{2,1,0:T(8,128)(2,1)}, bf16[8,64,128]{2,1,0:T(8,128)(2,1)S(1)}, u32[]{:S(2)}, u32[]{:S(2)}) collective-permute-start(bf16[8,64,128]{2,1,0:T(8,128)(2,1)} %get-tuple-element.38), channel_id=1, source_target_pairs={{0,6},{2,4},{4,2},{6,0},{1,7},{3,5},{5,3},{7,1},{8,14},{10,12},{12... | collective-permute-start | bytes 393224 | tf_op jit(solution)/shard_map/ppermute | solution.py:285
  154.5 23.0 %copy-start.2 = (bf16[8,64,128]{2,1,0:T(8,128)(2,1)S(1)}, bf16[8,64,128]{2,1,0:T(8,128)(2,1)}, u32[]{:S(2)}) copy-start(bf16[8,64,128]{2,1,0:T(8,128)(2,1)} %get-tuple-element.49.refs_0_) | copy-start | bytes 393220
  177.4 6.7 %copy-start.6 = (bf16[8,32,128]{2,1,0:T(8,128)(2,1)S(1)}, bf16[8,32,128]{2,1,0:T(8,128)(2,1)}, u32[]{:S(2)}) copy-start(bf16[8,32,128]{2,1,0:T(8,128)(2,1)} %get-tuple-element.46) | copy-start | bytes 196612
  177.4 8.8 %copy-start.5 = (bf16[8,32,128]{2,1,0:T(8,128)(2,1)S(1)}, bf16[8,32,128]{2,1,0:T(8,128)(2,1)}, u32[]{:S(2)}) copy-start(bf16[8,32,128]{2,1,0:T(8,128)(2,1)} %get-tuple-element.47) | copy-start | bytes 196612
  177.5 12.1 %copy-start.4 = (bf16[8,32,128]{2,1,0:T(8,128)(2,1)S(1)}, bf16[8,32,128]{2,1,0:T(8,128)(2,1)}, u32[]{:S(2)}) copy-start(bf16[8,32,128]{2,1,0:T(8,128)(2,1)} %get-tuple-element.48) | copy-start | bytes 196612
  177.5 19.1 %copy-start = (bf16[1,1,96,4096]{3,2,1,0:T(8,128)(2,1)S(1)}, bf16[1,1,96,4096]{3,2,1,0:T(8,128)(2,1)}, u32[]{:S(2)}) copy-start(bf16[1,1,96,4096]{3,2,1,0:T(8,128)(2,1)} %latents.3) | copy-start | bytes 2359300
  177.5 19.1 %copy-start.1 = (bf16[1,4096]{1,0:T(2,128)(2,1)S(1)}, bf16[1,4096]{1,0:T(2,128)(2,1)}, u32[]{:S(2)}) copy-start(bf16[1,4096]{1,0:T(2,128)(2,1)} %gain.3) | copy-start | bytes 24580
  178.4 21.3 %copy-start.3 = (bf16[8,32,128]{2,1,0:T(8,128)(2,1)S(1)}, bf16[8,32,128]{2,1,0:T(8,128)(2,1)}, u32[]{:S(2)}) copy-start(bf16[8,32,128]{2,1,0:T(8,128)(2,1)} %get-tuple-element.54.refs_0_) | copy-start | bytes 196612
  178.4 18.2 %all-to-all-start.2 = ((bf16[8,4,64,128]{3,2,1,0:T(8,128)(2,1)}), bf16[8,4,64,128]{3,2,1,0:T(8,128)(2,1)S(1)}, u32[]{:S(2)}, u32[]{:S(2)}) async-start(bf16[8,4,64,128]{3,2,1,0:T(8,128)(2,1)} %shard_map.90), calls=%async_computation.2 | async-start | bytes 1048576 | tf_op jit(solution)/shard_map/all_to_all | solution.py:281
  184.1 6.4 %collective-permute-start.3 = (bf16[8,32,128]{2,1,0:T(8,128)(2,1)S(1)}, bf16[8,32,128]{2,1,0:T(8,128)(2,1)S(1)}, u32[]{:S(2)}, u32[]{:S(2)}) collective-permute-start(bf16[8,32,128]{2,1,0:T(8,128)(2,1)S(1)} %copy-done.6), channel_id=1, source_target_pairs={{0,2},{2,0},{4,6},{6,4},{1,3},{3,1},{5,7},{7,5},{8,10},{10,8},{12,... | collective-permute-start | bytes 196616 | tf_op jit(solution)/shard_map/ppermute | solution.py:285
  186.2 7.2 %collective-permute-start.4 = (bf16[8,32,128]{2,1,0:T(8,128)(2,1)S(1)}, bf16[8,32,128]{2,1,0:T(8,128)(2,1)S(1)}, u32[]{:S(2)}, u32[]{:S(2)}) collective-permute-start(bf16[8,32,128]{2,1,0:T(8,128)(2,1)S(1)} %copy-done.5), channel_id=1, source_target_pairs={{0,4},{2,6},{4,0},{6,2},{1,5},{3,7},{5,1},{7,3},{8,12},{10,14},{12... | collective-permute-start | bytes 196616 | tf_op jit(solution)/shard_map/ppermute | solution.py:285
  189.5 7.0 %collective-permute-start.5 = (bf16[8,32,128]{2,1,0:T(8,128)(2,1)S(1)}, bf16[8,32,128]{2,1,0:T(8,128)(2,1)S(1)}, u32[]{:S(2)}, u32[]{:S(2)}) collective-permute-start(bf16[8,32,128]{2,1,0:T(8,128)(2,1)S(1)} %copy-done.4), channel_id=1, source_target_pairs={{0,6},{2,4},{4,2},{6,0},{1,7},{3,5},{5,3},{7,1},{8,14},{10,12},{12... | collective-permute-start | bytes 196616 | tf_op jit(solution)/shard_map/ppermute | solution.py:285
  196.9 21.5 %collective-permute-start.6 = (bf16[64,4096]{1,0:T(8,128)(2,1)S(1)}, bf16[64,4096]{1,0:T(8,128)(2,1)S(1)}, u32[]{:S(2)}, u32[]{:S(2)}) collective-permute-start(bf16[64,4096]{1,0:T(8,128)(2,1)S(1)} %shard_map.93.refs_2_), channel_id=1, source_target_pairs={{0,128},{128,0},{1,129},{129,1},{2,130},{130,2},{3,131},{131,3},{4... | collective-permute-start | bytes 1572872 | tf_op jit(solution)/shard_map/ppermute | solution.py:300
  211.5 6.8 %collective-permute-start.7 = (bf16[32,4096]{1,0:T(8,128)(2,1)S(1)}, bf16[32,4096]{1,0:T(8,128)(2,1)S(1)}, u32[]{:S(2)}, u32[]{:S(2)}) collective-permute-start(bf16[32,4096]{1,0:T(8,128)(2,1)S(1)} %shard_map.94.refs_3_), channel_id=1, source_target_pairs={{0,128},{128,0},{1,129},{129,1},{2,130},{130,2},{3,131},{131,3},{4... | collective-permute-start | bytes 786440 | tf_op jit(solution)/shard_map/ppermute | solution.py:300
where the time goes:
time: 221 us; the launch traced here: 219 us
  waiting for transfers between devices  102 us (46%)
  Pallas kernels  62.9 us (28%)
  starting transfers between devices  40.5 us (18%)
  blocking collectives  11.6 us (5%)
    all_to_all x3, waiting for transfers between devices, per_device(): lax.all_to_all(a, axes, split_axis=0, concat_axis=0, tiled=True)  91.4 us
    pallas_call x2, Pallas kernels, attend(): pl.pallas_call(functools.partial(attend_kernel, arrays=len(arrays), shard...  53.9 us
    all_to_all x3, starting transfers between devices, per_device(): lax.all_to_all(a, axes, split_axis=0, concat_axis=0, tiled=True)  26 us
    ppermute x6, starting transfers between devices, along_z(): lax.ppermute(p, Z, [(i, i ^ d) for i in range(FAR)])  11.7 us
    all_to_all x1, blocking collectives, per_device(): lax.all_to_all(a, axes, split_axis=0, concat_axis=0, tiled=True)  11.6 us
    ppermute x6, waiting for transfers between devices, along_z(): lax.ppermute(p, Z, [(i, i ^ d) for i in range(FAR)])  6.08 us
    pallas_call x2, Pallas kernels, pack(): pl.pallas_call(functools.partial(pack_kernel, spans=spans), in_specs=[pl....  5.24 us
    ppermute x2, waiting for transfers between devices, per_device(): swap = lambda a: lax.ppermute(a, 'expert', [(0, 1), (1, 0)])  4.71 us
  transfers between devices with their start and end apart: 11, of which 4 were waited for; matrix products, arithmetic and copies ran while one was open for 0% of the time, Pallas kernels for 26%

commit v1 on v0

--- a/solution.py
+++ b/solution.py
@@ -23,11 +23,15 @@
 SAFE_LOG2 = 100.0
 CONTRACT_LAST = (((1,), (1,)), ((), ()))
 VMEM_LIMIT = 32 << 20
-ATTEND_VMEM = 52 << 20
+ATTEND_VMEM = 40 << 20
 
 
 def in_vmem(a):
     return pltpu.with_memory_space_constraint(a, pltpu.VMEM)
+
+
+def in_hbm(a):
+    return pltpu.with_memory_space_constraint(a, pltpu.HBM)
 
 
 def sigma_of(step):
@@ -35,15 +39,12 @@
     return FLOW_SHIFT * level / (1.0 + (FLOW_SHIFT - 1.0) * level)
 
 
-def pack_kernel(*refs, spans):
-    count = len(spans)
+def pack_kernel(*refs, branch):
+    count = len(refs) - 5
     sources, out, (ins, outs, in_sems, out_sems) = refs[:count], refs[count], refs[count + 1 :]
-    heads = out.shape[0]
-    pieces, at = [], 0
-    for source, (first, rows) in zip(sources, spans):
-        for branch in range(2):
-            pieces.append((source.at[0, 0, branch, pl.ds(first, rows)], at, rows))
-            at += rows
+    heads, total, _ = out.shape
+    rows = total // count
+    pieces = [(source.at[0, 0, branch], n * rows, rows) for n, source in enumerate(sources)]
     reads = [
         pltpu.make_async_copy(source, ins.at[pl.ds(at, rows)], in_sems.at[n])
         for n, (source, at, rows) in enumerate(pieces)
@@ -63,13 +64,13 @@
         write.wait()
 
 
-def pack(sources, spans):
-    width = sources[0].shape[-1]
+def pack(branch, sources):
+    tokens, width = sources[0].shape[3:]
     heads = width // HDIM
-    total = sum(2 * rows for _, rows in spans)
-    count = 2 * len(spans)
+    count = len(sources)
+    total = count * tokens
     return pl.pallas_call(
-        functools.partial(pack_kernel, spans=spans),
+        functools.partial(pack_kernel, branch=branch),
         in_specs=[pl.BlockSpec(memory_space=pltpu.HBM) for _ in sources],
         out_specs=pl.BlockSpec(memory_space=pltpu.HBM),
         out_shape=pltpu.HBM((heads, total, HDIM), BF16),
@@ -80,43 +81,46 @@
             pltpu.SemaphoreType.DMA((count,)),
         ],
         compiler_params=pltpu.CompilerParams(vmem_limit_bytes=VMEM_LIMIT),
-    )(*(pltpu.with_memory_space_constraint(a, pltpu.HBM) for a in sources))
-
-
-def attend_kernel(place, *refs, arrays, shard, part, first, groups, normed):
-    kv_ref, q_ref = refs[0], refs[arrays - 1]
-    norms_in = refs[arrays] if normed else None
-    *outs, norms = refs[-FAR - 1 :]
-    peers = kv_ref.shape[0]
-    rows = groups * NEAR * part
+    )(*(in_hbm(a) for a in sources))
+
+
+def attend_kernel(place, kvq_ref, *refs, shard, part, first, groups, normed, guide):
+    refs = list(refs)
+    norm_in = refs.pop(0) if normed else None
+    cond_ref = refs.pop(0) if guide else None
+    *outs, norm = refs
+    peers = kvq_ref.shape[0]
+    chunks = 2
+    per_chunk = groups // chunks
+    rows = per_chunk * NEAR * part
+    step = pl.program_id(0)
 
     def resident(n, at=slice(None)):
-        return kv_ref[at, n * shard : (n + 1) * shard].reshape(-1, HDIM)
+        return kvq_ref[at, n * shard : (n + 1) * shard].reshape(-1, HDIM)
 
     def most(vectors):
         squares = jnp.dot(vectors * vectors, jnp.ones((HDIM, HDIM), BF16), preferred_element_type=F32)
         return jnp.max(squares) * 1.01
 
-    @pl.when(pl.program_id(0) == 0)
+    @pl.when(step == 0)
     def _():
-        for c in range(2):
-            norms[c] = norms_in[c] if normed else most(resident(c))
+        norm[0] = norm_in[0] if normed else most(resident(0))
 
     queries, bound = [], 0.0
-    for c in range(2):
-        own = slice(first + c * part, first + (c + 1) * part)
+    for c in range(chunks):
         pieces = []
-        for g in range(groups):
-            other = (pl.program_id(0) * groups + g) ^ place[0]
+        for g in range(per_chunk):
+            other = (step * groups + c * per_chunk + g) ^ place[0]
             for y in range(NEAR // 2):
-                pieces.append(q_ref[pl.ds(y * 2 * FAR + other * 2, 2), own])
+                at = pl.ds(y * 2 * FAR + other * 2, 2)
+                pieces.append(kvq_ref[at, 2 * shard + first : 2 * shard + first + part])
         q = jnp.concatenate(pieces, axis=0).reshape(rows, HDIM)
         queries.append(q)
-        bound = jnp.maximum(bound, most(q) * norms[c])
+        bound = jnp.maximum(bound, most(q) * norm[0])
     unshifted = bound <= (SAFE_LOG2 / LOG2_SCALE) ** 2
 
-    def scores(c, k):
-        return lax.dot_general(queries[c], k, CONTRACT_LAST, preferred_element_type=F32) * LOG2_SCALE
+    def scores(q, k):
+        return lax.dot_general(q, k, CONTRACT_LAST, preferred_element_type=F32) * LOG2_SCALE
 
     def lanes(weights):
         return sum(weights[:, at : at + HDIM] for at in range(0, weights.shape[1], HDIM))
@@ -124,65 +128,78 @@
     def weigh(weights, v):
         return jnp.dot(weights.astype(BF16), v, preferred_element_type=F32)
 
-    def finish(sums, totals):
-        cond, uncond = (s / jnp.sum(t, axis=1, keepdims=True) for s, t in zip(sums, totals))
-        guided = (uncond + GUIDANCE * (cond - uncond)).astype(BF16).reshape(groups, NEAR, part, HDIM)
-        for step in range(FAR // groups):
-
-            @pl.when(pl.program_id(0) == step)
-            def _():
-                for g in range(groups):
-                    outs[step * groups + g][...] = guided[g]
+    def finish(c, total, count):
+        attended = total / jnp.sum(count, axis=1, keepdims=True)
+        shape = (per_chunk, NEAR, part, HDIM)
+        if not guide:
+            outs[0][c * per_chunk : (c + 1) * per_chunk] = attended.reshape(shape)
+            return
+        cond = cond_ref[c * per_chunk : (c + 1) * per_chunk].reshape(rows, HDIM)
+        guided = (attended + GUIDANCE * (cond - attended)).astype(BF16).reshape(shape)
+        for d in range(FAR):
+            if d % groups // per_chunk == c:
+
+                @pl.when(step == d // groups)
+                def _():
+                    outs[d][...] = guided[d % per_chunk]
 
     @pl.when(unshifted)
     def _():
-        ahead = [scores(c, resident(c)) for c in range(2)]
+        ahead = [scores(q, resident(0)) for q in queries]
         weights = [jnp.exp2(a) for a in ahead]
-        finish([weigh(w, resident(2 + c)) for c, w in enumerate(weights)], [lanes(w) for w in weights])
+        sums = [weigh(w, resident(1)) for w in weights]
+        for c in range(chunks):
+            finish(c, sums[c], lanes(weights[c]))
 
     @pl.when(jnp.logical_not(unshifted))
     def _():
-        sums, totals = [], []
         per = 4
-        for c in range(2):
+        for c, q in enumerate(queries):
 
             def highest(j, m):
-                return jnp.maximum(m, jnp.max(scores(c, resident(c, pl.ds(j * per, per))), axis=1, keepdims=True))
+                return jnp.maximum(m, jnp.max(scores(q, resident(0, pl.ds(j * per, per))), axis=1, keepdims=True))
 
             top = lax.fori_loop(0, peers // per, highest, jnp.full((rows, 1), -jnp.inf, F32))
 
             def add(j, carry):
                 at = pl.ds(j * per, per)
-                weights = jnp.exp2(scores(c, resident(c, at)) - top)
-                return carry[0] + weigh(weights, resident(2 + c, at)), carry[1] + lanes(weights)
+                weights = jnp.exp2(scores(q, resident(0, at)) - top)
+                return carry[0] + weigh(weights, resident(1, at)), carry[1] + lanes(weights)
 
             zero = jnp.zeros((rows, HDIM), F32)
-            total, count = lax.fori_loop(0, peers // per, add, (zero, zero))
-            sums.append(total)
-            totals.append(count)
-        finish(sums, totals)
-
-
-def attend(place, arrays, shard, part, first, groups, norms=()):
+            finish(c, *lax.fori_loop(0, peers // per, add, (zero, zero)))
+
+
+def attend(place, kvq, part, first, groups, norm=(), cond=()):
     smem = pl.BlockSpec(memory_space=pltpu.SMEM)
     whole = pl.BlockSpec(memory_space=pltpu.VMEM)
-    *outs, norms = pl.pallas_call(
+    heads_spec = pl.BlockSpec(kvq.shape, lambda i: (0, 0, 0), pipeline_mode=pl.Buffered(1))
+    if cond:
+        heads_spec = whole
+        out_specs = [whole] * FAR
+        out_shape = [jax.ShapeDtypeStruct((NEAR, part, HDIM), BF16)] * FAR
+    else:
+        out_specs = [pl.BlockSpec((groups, NEAR, part, HDIM), lambda i: (i, 0, 0, 0))]
+        out_shape = [pltpu.HBM((FAR, NEAR, part, HDIM), F32)]
+    *outs, norm_out = pl.pallas_call(
         functools.partial(
             attend_kernel,
-            arrays=len(arrays),
-            shard=shard,
+            shard=kvq.shape[1] // 3,
             part=part,
             first=first,
             groups=groups,
-            normed=bool(norms),
+            normed=bool(norm),
+            guide=bool(cond),
         ),
         grid=(FAR // groups,),
-        in_specs=[smem] + [whole for _ in arrays] + [smem for _ in norms],
-        out_specs=[whole] * FAR + [smem],
-        out_shape=[jax.ShapeDtypeStruct((NEAR, part, HDIM), BF16)] * FAR + [jax.ShapeDtypeStruct((2,), F32)],
+        in_specs=[smem, heads_spec]
+        + [smem for _ in norm]
+        + [pl.BlockSpec((groups, NEAR, part, HDIM), lambda i: (i, 0, first // part, 0)) for _ in cond],
+        out_specs=out_specs + [smem],
+        out_shape=out_shape + [jax.ShapeDtypeStruct((1,), F32)],
         compiler_params=pltpu.CompilerParams(vmem_limit_bytes=ATTEND_VMEM),
-    )(place, *(in_vmem(a) for a in arrays), *norms)
-    return outs, norms
+    )(place, in_vmem(kvq) if cond else in_hbm(kvq), *norm, *(in_hbm(a) for a in cond))
+    return outs, norm_out
 
 
 def regroup_kernel(*refs):
@@ -284,13 +301,14 @@
     def along_z(pieces):
         return [lax.ppermute(p, Z, [(i, i ^ d) for i in range(FAR)]) if d else p for d, p in enumerate(pieces)]
 
-    kvq = exchange(pack((keys, values, queries), ((0, tokens), (0, tokens), (0, head))), SEQ)
-    rest, _ = together((pack((queries,), ((head, tail),)), kvq))
-    rest = exchange(rest, SEQ)
-    own, norms = attend(place, (kvq,), tokens, head, 4 * tokens, groups=2)
-    own, rest = together((own, rest))
+    sources = (keys, values, queries)
+    cond_kvq = exchange(pack(0, sources), SEQ)
+    packed, _ = together((pack(1, sources), cond_kvq))
+    kvq = exchange(packed, SEQ)
+    cond, _ = attend(place, cond_kvq, tokens, 0, groups=2)
+    own, norm = attend(place, kvq, head, 0, groups=2, cond=cond)
     near = along_z(own)
-    own, _ = attend(place, (kvq, rest), tokens, tail, 0, groups=4, norms=(norms,))
+    own, _ = attend(place, kvq, tail, head, groups=4, norm=(norm,), cond=cond)
     near, own = together((near, own))
     far = along_z(own)
     guided_head = exchange(regroup(near), (Y, CORE))

time: 221 us -> 218 us (0.986); the launches traced: 219 us -> 219 us
  waiting for transfers between devices: 102 us -> 81.9 us
  Pallas kernels: 62.9 us -> 82.5 us
  starting transfers between devices: 40.5 us -> 37.9 us
    all_to_all x3, waiting for transfers between devices: 91.4 us -> 65.5 us  [per_device(): lax.all_to_all(a, axes, split_axis=0, concat_axis=0, tiled=True)]
    pallas_call x4 -> x5, Pallas kernels: 59.1 us -> 78.7 us  [the longest x3 73.2 us: attend(): pl.pallas_call(functools.partial(attend_kernel, shard=kvq.shape[1] // 3,...]
    ppermute x6, waiting for transfers between devices: 6.08 us -> 11.7 us  [along_z(): lax.ppermute(p, Z, [(i, i ^ d) for i in range(FAR)])]
    all_to_all x3, starting transfers between devices: 26 us -> 23.4 us  [per_device(): lax.all_to_all(a, axes, split_axis=0, concat_axis=0, tiled=True)]
  transfers between devices with their start and end apart: 11 -> 11, of which waited for: 4 -> 7; matrix products, arithmetic and copies ran while one was open for 0% -> 0% of each run, Pallas kernels for 26% -> 22%
where the time goes in v1:
time: 218 us; the launch traced here: 219 us
  Pallas kernels  82.5 us (38%)
  waiting for transfers between devices  81.9 us (38%)
  starting transfers between devices  37.9 us (17%)
  blocking collectives  12.8 us (6%)
    pallas_call x3, Pallas kernels, attend(): pl.pallas_call(functools.partial(attend_kernel, shard=kvq.shape[1] // 3,...  73.2 us
    all_to_all x3, waiting for transfers between devices, per_device(): lax.all_to_all(a, axes, split_axis=0, concat_axis=0, tiled=True)  65.5 us
    all_to_all x3, starting transfers between devices, per_device(): lax.all_to_all(a, axes, split_axis=0, concat_axis=0, tiled=True)  23.4 us
    all_to_all x1, blocking collectives, per_device(): lax.all_to_all(a, axes, split_axis=0, concat_axis=0, tiled=True)  12.8 us
    ppermute x6, starting transfers between devices, along_z(): lax.ppermute(p, Z, [(i, i ^ d) for i in range(FAR)])  12 us
    ppermute x6, waiting for transfers between devices, along_z(): lax.ppermute(p, Z, [(i, i ^ d) for i in range(FAR)])  11.7 us
    pallas_call x2, Pallas kernels, pack(): pl.pallas_call(functools.partial(pack_kernel, branch=branch), in_specs=[p...  5.49 us
    ppermute x2, waiting for transfers between devices, per_device(): swap = lambda a: lax.ppermute(a, 'expert', [(0, 1), (1, 0)])  4.71 us
  transfers between devices with their start and end apart: 11, of which 7 were waited for; matrix products, arithmetic and copies ran while one was open for 0% of the time, Pallas kernels for 22%

profile of v1, /device:TPU:1, one launch (start us, length us, event | category | flops | bytes accessed | tf_op | source)
XLA Modules:
  0.0 218.6 jit_solution(14866759502543868910)
XLA Ops:
  0.6 2.8 %shard_map.87 = bf16[32,288,128]{2,1,0:T(8,128)(2,1)} custom-call(bf16[1,1,2,96,4096]{4,3,2,1,0:T(8,128)(2,1)} %refs_0_.3, bf16[1,1,2,96,4096]{4,3,2,1,0:T(8,128)(2,1)} %refs_1_.3, bf16[1,1,2,96,4096]{4,3,2,1,0:T(8,128)(2,1)} %refs_2_.4), custom_call_target="tpu_custom_call" | custom-call | tf_op jit(solution)/shard_map/pallas_call | solution.py:72
  3.4 12.8 %all-to-all-start = ((bf16[32,288,128]{2,1,0:T(8,128)(2,1)}), bf16[32,288,128]{2,1,0:T(8,128)(2,1)S(1)}, u32[]{:S(2)}, u32[]{:S(2)}) async-start(bf16[32,288,128]{2,1,0:T(8,128)(2,1)} %shard_map.87), calls=%async_computation | async-start | bytes 4718592 | tf_op jit(solution)/shard_map/all_to_all | solution.py:298
  16.2 2.7 %shard_map.86 = bf16[32,288,128]{2,1,0:T(8,128)(2,1)} custom-call(bf16[1,1,2,96,4096]{4,3,2,1,0:T(8,128)(2,1)} %refs_0_.3, bf16[1,1,2,96,4096]{4,3,2,1,0:T(8,128)(2,1)} %refs_1_.3, bf16[1,1,2,96,4096]{4,3,2,1,0:T(8,128)(2,1)} %refs_2_.4), custom_call_target="tpu_custom_call" | custom-call | tf_op jit(solution)/shard_map/pallas_call | solution.py:72
  18.9 53.1 %all-to-all-done.kvq_ref = bf16[32,288,128]{2,1,0:T(8,128)(2,1)S(1)} async-done(((bf16[32,288,128]{2,1,0:T(8,128)(2,1)}), bf16[32,288,128]{2,1,0:T(8,128)(2,1)S(1)}, u32[]{:S(2)}, u32[]{:S(2)}) %all-to-all-start) | async-done | bytes 2359328 | tf_op jit(solution)/shard_map/all_to_all | solution.py:298
  72.1 0.0 copy-start.2
  72.1 1.4 copy-done.2
  73.5 6.0 %all-to-all-start.1 = ((bf16[32,288,128]{2,1,0:T(8,128)(2,1)}), bf16[32,288,128]{2,1,0:T(8,128)(2,1)S(1)}, u32[]{:S(2)}, u32[]{:S(2)}) async-start(bf16[32,288,128]{2,1,0:T(8,128)(2,1)} %shard_map.86), calls=%async_computation.1 | async-start | bytes 4718592 | tf_op jit(solution)/shard_map/all_to_all | solution.py:298
  79.5 36.9 %shard_map.88 = (f32[4,8,96,128]{3,2,1,0:T(8,128)}, f32[1]{0:T(128)}) custom-call(s32[1]{0:T(128)} %bitcast.place, bf16[32,288,128]{2,1,0:T(8,128)(2,1)} %copy-done.2), custom_call_target="tpu_custom_call" | custom-call | tf_op jit(solution)/shard_map/pallas_call | solution.py:184
  116.4 12.4 %all-to-all-done.1.kvq_ref = bf16[32,288,128]{2,1,0:T(8,128)(2,1)S(1)} async-done(((bf16[32,288,128]{2,1,0:T(8,128)(2,1)}), bf16[32,288,128]{2,1,0:T(8,128)(2,1)S(1)}, u32[]{:S(2)}, u32[]{:S(2)}) %all-to-all-start.1) | async-done | bytes 2359328 | tf_op jit(solution)/shard_map/all_to_all | solution.py:298
  128.8 30.2 %shard_map.89 = (bf16[8,64,128]{2,1,0:T(8,128)(2,1)S(1)}, bf16[8,64,128]{2,1,0:T(8,128)(2,1)S(1)}, bf16[8,64,128]{2,1,0:T(8,128)(2,1)S(1)}, bf16[8,64,128]{2,1,0:T(8,128)(2,1)S(1)}, f32[1]{0:T(128)}) custom-call(s32[1]{0:T(128)} %bitcast.place, bf16[32,288,128]{2,1,0:T(8,128)(2,1)S(1)} %all-to-all-done.1.kvq_ref, ...), custom_call_target="tpu_custom_call" | custom-call | tf_op jit(solution)/shard_map/pallas_call | solution.py:184
  158.9 0.1 collective-permute-start
  159.0 6.3 %collective-permute-start.1 = (bf16[8,64,128]{2,1,0:T(8,128)(2,1)S(1)}, bf16[8,64,128]{2,1,0:T(8,128)(2,1)S(1)}, u32[]{:S(2)}, u32[]{:S(2)}) collective-permute-start(bf16[8,64,128]{2,1,0:T(8,128)(2,1)S(1)} %get-tuple-element.30), channel_id=1, source_target_pairs={{0,4},{2,6},{4,0},{6,2},{1,5},{3,7},{5,1},{7,3},{8,12},{10,14},{12... | collective-permute-start | bytes 393224 | tf_op jit(solution)/shard_map/ppermute | solution.py:302
  165.3 0.0 collective-permute-start.2
  165.3 0.0 copy-start
  165.3 0.0 copy-start.1
  165.3 6.1 %shard_map.90 = (bf16[8,32,128]{2,1,0:T(8,128)(2,1)S(1)}, bf16[8,32,128]{2,1,0:T(8,128)(2,1)S(1)}, bf16[8,32,128]{2,1,0:T(8,128)(2,1)S(1)}, bf16[8,32,128]{2,1,0:T(8,128)(2,1)S(1)}, f32[1]{0:T(128)}) custom-call(s32[1]{0:T(128)} %bitcast.place, bf16[32,288,128]{2,1,0:T(8,128)(2,1)S(1)} %all-to-all-done.1.kvq_ref, f32[1]{0:T(128)} %get-tuple-element.32.refs_0_, ...), custom_call_target="tpu_custom_call" | custom-call | tf_op jit(solution)/shard_map/pallas_call | solution.py:184
  171.4 0.0 collective-permute-done.refs_1_
  171.4 1.5 collective-permute-done.1.refs_2_
  172.9 4.6 %collective-permute-done.2.refs_3_ = bf16[8,64,128]{2,1,0:T(8,128)(2,1)S(1)} collective-permute-done((bf16[8,64,128]{2,1,0:T(8,128)(2,1)S(1)}, bf16[8,64,128]{2,1,0:T(8,128)(2,1)S(1)}, u32[]{:S(2)}, u32[]{:S(2)}) %collective-permute-start.2) | collective-permute-done | bytes 131104 | tf_op jit(solution)/shard_map/ppermute | solution.py:302
  177.5 0.8 shard_map.91
  178.3 4.6 %all-to-all-start.2 = ((bf16[8,4,64,128]{3,2,1,0:T(8,128)(2,1)}), bf16[8,4,64,128]{3,2,1,0:T(8,128)(2,1)S(1)}, u32[]{:S(2)}, u32[]{:S(2)}) async-start(bf16[8,4,64,128]{3,2,1,0:T(8,128)(2,1)} %shard_map.91), calls=%async_computation.2 | async-start | bytes 1048576 | tf_op jit(solution)/shard_map/all_to_all | solution.py:298
  183.0 0.0 collective-permute-start.3
  183.0 2.0 collective-permute-start.4
  184.9 3.7 %collective-permute-start.5 = (bf16[8,32,128]{2,1,0:T(8,128)(2,1)S(1)}, bf16[8,32,128]{2,1,0:T(8,128)(2,1)S(1)}, u32[]{:S(2)}, u32[]{:S(2)}) collective-permute-start(bf16[8,32,128]{2,1,0:T(8,128)(2,1)S(1)} %get-tuple-element.40), channel_id=1, source_target_pairs={{0,6},{2,4},{4,2},{6,0},{1,7},{3,5},{5,3},{7,1},{8,14},{10,12},{12... | collective-permute-start | bytes 196616 | tf_op jit(solution)/shard_map/ppermute | solution.py:302
  189.3 0.0 collective-permute-done.3.refs_1_
  189.3 0.8 collective-permute-done.4.refs_2_
  190.0 4.9 %collective-permute-done.5.refs_3_ = bf16[8,32,128]{2,1,0:T(8,128)(2,1)S(1)} collective-permute-done((bf16[8,32,128]{2,1,0:T(8,128)(2,1)S(1)}, bf16[8,32,128]{2,1,0:T(8,128)(2,1)S(1)}, u32[]{:S(2)}, u32[]{:S(2)}) %collective-permute-start.5) | collective-permute-done | bytes 65568 | tf_op jit(solution)/shard_map/ppermute | solution.py:302
  194.9 0.0 all-to-all-done.2.refs_0_.guided
  194.9 0.0 copy-done
  194.9 0.0 copy-done.1
  194.9 0.4 shard_map.94.refs_2_
  195.3 2.4 %collective-permute-start.6 = (bf16[64,4096]{1,0:T(8,128)(2,1)S(1)}, bf16[64,4096]{1,0:T(8,128)(2,1)S(1)}, u32[]{:S(2)}, u32[]{:S(2)}) collective-permute-start(bf16[64,4096]{1,0:T(8,128)(2,1)S(1)} %shard_map.94.refs_2_), channel_id=1, source_target_pairs={{0,128},{128,0},{1,129},{129,1},{2,130},{130,2},{3,131},{131,3},{4... | collective-permute-start | bytes 1572872 | tf_op jit(solution)/shard_map/ppermute | solution.py:318
  197.7 12.8 %all_to_all.20.refs_1_.guided = bf16[8,4,32,128]{3,2,1,0:T(8,128)(2,1)S(1)} all-to-all(bf16[8,4,32,128]{3,2,1,0:T(8,128)(2,1)S(1)} %shard_map.92), channel_id=1, replica_groups=mesh['expert'=2,'batch'=4,'seq_y'=4,'seq_z'=4,'seq_core'=2] {'seq_y','se..., dimensions={0} | all-to-all | bytes 524288 | tf_op jit(solution)/shard_map/all_to_all | solution.py:298
  210.5 0.2 shard_map.95.refs_3_
  210.8 0.1 collective-permute-start.7
  211.5 1.4 shard_map.93
  212.9 4.7 %collective-permute-done.7.refs_1_ = bf16[32,4096]{1,0:T(8,128)(2,1)S(1)} collective-permute-done((bf16[32,4096]{1,0:T(8,128)(2,1)S(1)}, bf16[32,4096]{1,0:T(8,128)(2,1)S(1)}, u32[]{:S(2)}, u32[]{:S(2)}) %collective-permute-start.7) | collective-permute-done | bytes 262176 | tf_op jit(solution)/shard_map/ppermute | solution.py:318
  217.6 0.0 collective-permute-done.6.refs_0_
  217.6 1.0 shard_map.96
  (1 shorter events, 0.0 us)
Async XLA Ops:
  3.4 68.6 %all-to-all-start = ((bf16[32,288,128]{2,1,0:T(8,128)(2,1)}), bf16[32,288,128]{2,1,0:T(8,128)(2,1)S(1)}, u32[]{:S(2)}, u32[]{:S(2)}) async-start(bf16[32,288,128]{2,1,0:T(8,128)(2,1)} %shard_map.87), calls=%async_computation | async-start | bytes 4718592 | tf_op jit(solution)/shard_map/all_to_all | solution.py:298
  72.1 1.4 copy-start.2
  73.5 55.3 %all-to-all-start.1 = ((bf16[32,288,128]{2,1,0:T(8,128)(2,1)}), bf16[32,288,128]{2,1,0:T(8,128)(2,1)S(1)}, u32[]{:S(2)}, u32[]{:S(2)}) async-start(bf16[32,288,128]{2,1,0:T(8,128)(2,1)} %shard_map.86), calls=%async_computation.1 | async-start | bytes 4718592 | tf_op jit(solution)/shard_map/all_to_all | solution.py:298
  158.9 12.5 %collective-permute-start = (bf16[8,64,128]{2,1,0:T(8,128)(2,1)S(1)}, bf16[8,64,128]{2,1,0:T(8,128)(2,1)S(1)}, u32[]{:S(2)}, u32[]{:S(2)}) collective-permute-start(bf16[8,64,128]{2,1,0:T(8,128)(2,1)S(1)} %get-tuple-element.29), channel_id=1, source_target_pairs={{0,2},{2,0},{4,6},{6,4},{1,3},{3,1},{5,7},{7,5},{8,10},{10,8},{12,... | collective-permute-start | bytes 393224 | tf_op jit(solution)/shard_map/ppermute | solution.py:302
  159.0 13.9 %collective-permute-start.1 = (bf16[8,64,128]{2,1,0:T(8,128)(2,1)S(1)}, bf16[8,64,128]{2,1,0:T(8,128)(2,1)S(1)}, u32[]{:S(2)}, u32[]{:S(2)}) collective-permute-start(bf16[8,64,128]{2,1,0:T(8,128)(2,1)S(1)} %get-tuple-element.30), channel_id=1, source_target_pairs={{0,4},{2,6},{4,0},{6,2},{1,5},{3,7},{5,1},{7,3},{8,12},{10,14},{12... | collective-permute-start | bytes 393224 | tf_op jit(solution)/shard_map/ppermute | solution.py:302
  165.3 12.2 %collective-permute-start.2 = (bf16[8,64,128]{2,1,0:T(8,128)(2,1)S(1)}, bf16[8,64,128]{2,1,0:T(8,128)(2,1)S(1)}, u32[]{:S(2)}, u32[]{:S(2)}) collective-permute-start(bf16[8,64,128]{2,1,0:T(8,128)(2,1)S(1)} %get-tuple-element.31), channel_id=1, source_target_pairs={{0,6},{2,4},{4,2},{6,0},{1,7},{3,5},{5,3},{7,1},{8,14},{10,12},{12... | collective-permute-start | bytes 393224 | tf_op jit(solution)/shard_map/ppermute | solution.py:302
  165.3 29.6 %copy-start = (bf16[1,1,96,4096]{3,2,1,0:T(8,128)(2,1)S(1)}, bf16[1,1,96,4096]{3,2,1,0:T(8,128)(2,1)}, u32[]{:S(2)}) copy-start(bf16[1,1,96,4096]{3,2,1,0:T(8,128)(2,1)} %latents.3) | copy-start | bytes 2359300
  165.3 29.6 %copy-start.1 = (bf16[1,4096]{1,0:T(2,128)(2,1)S(1)}, bf16[1,4096]{1,0:T(2,128)(2,1)}, u32[]{:S(2)}) copy-start(bf16[1,4096]{1,0:T(2,128)(2,1)} %gain.3) | copy-start | bytes 24580
  178.3 16.5 %all-to-all-start.2 = ((bf16[8,4,64,128]{3,2,1,0:T(8,128)(2,1)}), bf16[8,4,64,128]{3,2,1,0:T(8,128)(2,1)S(1)}, u32[]{:S(2)}, u32[]{:S(2)}) async-start(bf16[8,4,64,128]{3,2,1,0:T(8,128)(2,1)} %shard_map.91), calls=%async_computation.2 | async-start | bytes 1048576 | tf_op jit(solution)/shard_map/all_to_all | solution.py:298
  183.0 6.3 %collective-permute-start.3 = (bf16[8,32,128]{2,1,0:T(8,128)(2,1)S(1)}, bf16[8,32,128]{2,1,0:T(8,128)(2,1)S(1)}, u32[]{:S(2)}, u32[]{:S(2)}) collective-permute-start(bf16[8,32,128]{2,1,0:T(8,128)(2,1)S(1)} %get-tuple-element.38), channel_id=1, source_target_pairs={{0,2},{2,0},{4,6},{6,4},{1,3},{3,1},{5,7},{7,5},{8,10},{10,8},{12,... | collective-permute-start | bytes 196616 | tf_op jit(solution)/shard_map/ppermute | solution.py:302
  183.0 7.1 %collective-permute-start.4 = (bf16[8,32,128]{2,1,0:T(8,128)(2,1)S(1)}, bf16[8,32,128]{2,1,0:T(8,128)(2,1)S(1)}, u32[]{:S(2)}, u32[]{:S(2)}) collective-permute-start(bf16[8,32,128]{2,1,0:T(8,128)(2,1)S(1)} %get-tuple-element.39), channel_id=1, source_target_pairs={{0,4},{2,6},{4,0},{6,2},{1,5},{3,7},{5,1},{7,3},{8,12},{10,14},{12... | collective-permute-start | bytes 196616 | tf_op jit(solution)/shard_map/ppermute | solution.py:302
  184.9 10.0 %collective-permute-start.5 = (bf16[8,32,128]{2,1,0:T(8,128)(2,1)S(1)}, bf16[8,32,128]{2,1,0:T(8,128)(2,1)S(1)}, u32[]{:S(2)}, u32[]{:S(2)}) collective-permute-start(bf16[8,32,128]{2,1,0:T(8,128)(2,1)S(1)} %get-tuple-element.40), channel_id=1, source_target_pairs={{0,6},{2,4},{4,2},{6,0},{1,7},{3,5},{5,3},{7,1},{8,14},{10,12},{12... | collective-permute-start | bytes 196616 | tf_op jit(solution)/shard_map/ppermute | solution.py:302
  195.3 22.3 %collective-permute-start.6 = (bf16[64,4096]{1,0:T(8,128)(2,1)S(1)}, bf16[64,4096]{1,0:T(8,128)(2,1)S(1)}, u32[]{:S(2)}, u32[]{:S(2)}) collective-permute-start(bf16[64,4096]{1,0:T(8,128)(2,1)S(1)} %shard_map.94.refs_2_), channel_id=1, source_target_pairs={{0,128},{128,0},{1,129},{129,1},{2,130},{130,2},{3,131},{131,3},{4... | collective-permute-start | bytes 1572872 | tf_op jit(solution)/shard_map/ppermute | solution.py:318
  210.8 6.8 %collective-permute-start.7 = (bf16[32,4096]{1,0:T(8,128)(2,1)S(1)}, bf16[32,4096]{1,0:T(8,128)(2,1)S(1)}, u32[]{:S(2)}, u32[]{:S(2)}) collective-permute-start(bf16[32,4096]{1,0:T(8,128)(2,1)S(1)} %shard_map.95.refs_3_), channel_id=1, source_target_pairs={{0,128},{128,0},{1,129},{129,1},{2,130},{130,2},{3,131},{131,3},{4... | collective-permute-start | bytes 786440 | tf_op jit(solution)/shard_map/ppermute | solution.py:318

commit v2 on v0

--- a/solution.py
+++ b/solution.py
@@ -83,10 +83,10 @@
     )(*(pltpu.with_memory_space_constraint(a, pltpu.HBM) for a in sources))
 
 
-def attend_kernel(place, *refs, arrays, shard, part, first, groups, normed):
+def attend_kernel(place, *refs, arrays, shard, part, first, steps, groups, nearest, normed):
     kv_ref, q_ref = refs[0], refs[arrays - 1]
     norms_in = refs[arrays] if normed else None
-    *outs, norms = refs[-FAR - 1 :]
+    *outs, norms = refs[arrays + normed :]
     peers = kv_ref.shape[0]
     rows = groups * NEAR * part
 
@@ -107,7 +107,7 @@
         own = slice(first + c * part, first + (c + 1) * part)
         pieces = []
         for g in range(groups):
-            other = (pl.program_id(0) * groups + g) ^ place[0]
+            other = (nearest + pl.program_id(0) * groups + g) ^ place[0]
             for y in range(NEAR // 2):
                 pieces.append(q_ref[pl.ds(y * 2 * FAR + other * 2, 2), own])
         q = jnp.concatenate(pieces, axis=0).reshape(rows, HDIM)
@@ -127,7 +127,7 @@
     def finish(sums, totals):
         cond, uncond = (s / jnp.sum(t, axis=1, keepdims=True) for s, t in zip(sums, totals))
         guided = (uncond + GUIDANCE * (cond - uncond)).astype(BF16).reshape(groups, NEAR, part, HDIM)
-        for step in range(FAR // groups):
+        for step in range(steps):
 
             @pl.when(pl.program_id(0) == step)
             def _():
@@ -163,9 +163,10 @@
         finish(sums, totals)
 
 
-def attend(place, arrays, shard, part, first, groups, norms=()):
+def attend(place, arrays, shard, part, first, span, groups, norms=()):
     smem = pl.BlockSpec(memory_space=pltpu.SMEM)
     whole = pl.BlockSpec(memory_space=pltpu.VMEM)
+    nearest, count = span
     *outs, norms = pl.pallas_call(
         functools.partial(
             attend_kernel,
@@ -173,13 +174,15 @@
             shard=shard,
             part=part,
             first=first,
+            steps=count // groups,
             groups=groups,
-            normed=bool(norms),
+            nearest=nearest,
+            normed=len(norms),
         ),
-        grid=(FAR // groups,),
+        grid=(count // groups,),
         in_specs=[smem] + [whole for _ in arrays] + [smem for _ in norms],
-        out_specs=[whole] * FAR + [smem],
-        out_shape=[jax.ShapeDtypeStruct((NEAR, part, HDIM), BF16)] * FAR + [jax.ShapeDtypeStruct((2,), F32)],
+        out_specs=[whole] * count + [smem],
+        out_shape=[jax.ShapeDtypeStruct((NEAR, part, HDIM), BF16)] * count + [jax.ShapeDtypeStruct((2,), F32)],
         compiler_params=pltpu.CompilerParams(vmem_limit_bytes=ATTEND_VMEM),
     )(place, *(in_vmem(a) for a in arrays), *norms)
     return outs, norms
@@ -275,31 +278,33 @@
 
 def per_device(queries, keys, values, latents, gain, steps_table, flags):
     tokens, width = queries.shape[3:]
-    tail = tokens // 3
-    head = tokens - tail
+    half = tokens // 2
     place = lax.axis_index(Z).reshape(1).astype(jnp.int32)
     exchange = lambda a, axes: lax.all_to_all(a, axes, split_axis=0, concat_axis=0, tiled=True)
     together = lax.optimization_barrier
 
-    def along_z(pieces):
-        return [lax.ppermute(p, Z, [(i, i ^ d) for i in range(FAR)]) if d else p for d, p in enumerate(pieces)]
-
-    kvq = exchange(pack((keys, values, queries), ((0, tokens), (0, tokens), (0, head))), SEQ)
-    rest, _ = together((pack((queries,), ((head, tail),)), kvq))
+    def along_z(pieces, nearest=0):
+        routes = [[(i, i ^ d) for i in range(FAR)] for d in range(nearest, nearest + len(pieces))]
+        return [p if r[0] == (0, 0) else lax.ppermute(p, Z, r) for p, r in zip(pieces, routes)]
+
+    kvq = exchange(pack((keys, values, queries), ((0, tokens), (0, tokens), (0, half))), SEQ)
+    rest, _ = together((pack((queries,), ((half, half),)), kvq))
     rest = exchange(rest, SEQ)
-    own, norms = attend(place, (kvq,), tokens, head, 4 * tokens, groups=2)
-    own, rest = together((own, rest))
+    own, norms = attend(place, (kvq,), tokens, half, 4 * tokens, (0, FAR), groups=2)
     near = along_z(own)
-    own, _ = attend(place, (kvq, rest), tokens, tail, 0, groups=4, norms=(norms,))
-    near, own = together((near, own))
-    far = along_z(own)
+    other = lambda nearest: attend(
+        place, (kvq, rest), tokens, half, 0, (nearest, FAR // 2), groups=2, norms=(norms,)
+    )[0]
+    far_low = other(0)
+    near, far_low = together((near, far_low))
     guided_head = exchange(regroup(near), (Y, CORE))
+    far = along_z(far_low) + along_z(other(FAR // 2), FAR // 2)
     far, guided_head = together((far, guided_head))
     guided_tail = exchange(regroup(far), (Y, CORE))
 
     swap = lambda a: lax.ppermute(a, "expert", [(0, 1), (1, 0)])
     moved, partner = [], []
-    for first, guided in ((0, guided_head), (head, guided_tail)):
+    for first, guided in ((0, guided_head), (half, guided_tail)):
         shape = (guided.shape[2], width)
         kernel = functools.partial(move_kernel, first=first)
         moved.append(update(kernel, shape, place, steps_table, (guided,), latents, gain))

time: 221 us -> 223 us (level)
  starting transfers between devices: 40.5 us -> 53.7 us
  blocking collectives: 11.6 us -> 0 us
    all_to_all x1 -> x0, blocking collectives: 11.6 us -> none  [per_device(): lax.all_to_all(a, axes, split_axis=0, concat_axis=0, tiled=True)]
    ppermute x2, starting transfers between devices: 2.84 us -> 10.5 us  [per_device(): swap = lambda a: lax.ppermute(a, 'expert', [(0, 1), (1, 0)])]
    all_to_all x3 -> x4, starting transfers between devices: 26 us -> 31.5 us  [per_device(): lax.all_to_all(a, axes, split_axis=0, concat_axis=0, tiled=True)]
    all_to_all x3 -> x4, waiting for transfers between devices: 91.4 us -> 87.5 us  [per_device(): lax.all_to_all(a, axes, split_axis=0, concat_axis=0, tiled=True)]
    ppermute x2, waiting for transfers between devices: 4.71 us -> 8.48 us  [per_device(): swap = lambda a: lax.ppermute(a, 'expert', [(0, 1), (1, 0)])]
    pallas_call x2 -> x3, Pallas kernels: 53.9 us -> 54.5 us  [attend(): pl.pallas_call(functools.partial(attend_kernel, arrays=len(arrays), shard...]
  transfers between devices with their start and end apart: 11 -> 12, of which waited for: 4 -> 7; matrix products, arithmetic and copies ran while one was open for 0% -> 0% of each run, Pallas kernels for 26% -> 26%
where the time goes in v2:
time: 223 us; the launch traced here: 224 us
  waiting for transfers between devices  104 us (47%)
  Pallas kernels  64.2 us (29%)
  starting transfers between devices  53.7 us (24%)
    all_to_all x4, waiting for transfers between devices, per_device(): lax.all_to_all(a, axes, split_axis=0, concat_axis=0, tiled=True)  87.5 us
    pallas_call x3, Pallas kernels, attend(): pl.pallas_call(functools.partial(attend_kernel, arrays=len(arrays), shard...  54.5 us
    all_to_all x4, starting transfers between devices, per_device(): lax.all_to_all(a, axes, split_axis=0, concat_axis=0, tiled=True)  31.5 us
    ppermute x6, starting transfers between devices, along_z(): lax.ppermute(p, Z, r)  11.6 us
    ppermute x2, starting transfers between devices, per_device(): swap = lambda a: lax.ppermute(a, 'expert', [(0, 1), (1, 0)])  10.5 us
    ppermute x2, waiting for transfers between devices, per_device(): swap = lambda a: lax.ppermute(a, 'expert', [(0, 1), (1, 0)])  8.48 us
    ppermute x6, waiting for transfers between devices, along_z(): lax.ppermute(p, Z, r)  7.53 us
    pallas_call x2, Pallas kernels, pack(): pl.pallas_call(functools.partial(pack_kernel, spans=spans), in_specs=[pl....  5.26 us
  transfers between devices with their start and end apart: 12, of which 7 were waited for; matrix products, arithmetic and copies ran while one was open for 0% of the time, Pallas kernels for 26%

profile of v2, /device:TPU:1, one launch (start us, length us, event | category | flops | bytes accessed | tf_op | source)
XLA Modules:
  0.0 223.5 jit_solution(8309548458291902042)
XLA Ops:
  0.6 3.3 %shard_map.86 = bf16[32,480,128]{2,1,0:T(8,128)(2,1)} custom-call(bf16[1,1,2,96,4096]{4,3,2,1,0:T(8,128)(2,1)} %refs_0_.2, bf16[1,1,2,96,4096]{4,3,2,1,0:T(8,128)(2,1)} %refs_1_.1, bf16[1,1,2,96,4096]{4,3,2,1,0:T(8,128)(2,1)} %refs_0_.3), custom_call_target="tpu_custom_call" | custom-call | tf_op jit(solution)/shard_map/pallas_call | solution.py:71
  3.9 12.8 %all-to-all-start = ((bf16[32,480,128]{2,1,0:T(8,128)(2,1)}), bf16[32,480,128]{2,1,0:T(8,128)(2,1)}, u32[]{:S(2)}, u32[]{:S(2)}) async-start(bf16[32,480,128]{2,1,0:T(8,128)(2,1)} %shard_map.86), calls=%async_computation | async-start | bytes 7864320 | tf_op jit(solution)/shard_map/all_to_all | solution.py:283
  16.7 2.0 shard_map.88
  18.7 85.0 %all-to-all-done.refs_0_ = bf16[32,480,128]{2,1,0:T(8,128)(2,1)} async-done(((bf16[32,480,128]{2,1,0:T(8,128)(2,1)}), bf16[32,480,128]{2,1,0:T(8,128)(2,1)}, u32[]{:S(2)}, u32[]{:S(2)}) %all-to-all-start) | async-done | bytes 3932192 | tf_op jit(solution)/shard_map/all_to_all | solution.py:283
  103.7 8.5 %all-to-all-start.1 = ((bf16[32,96,128]{2,1,0:T(8,128)(2,1)}), bf16[32,96,128]{2,1,0:T(8,128)(2,1)S(1)}, u32[]{:S(2)}, u32[]{:S(2)}) async-start(bf16[32,96,128]{2,1,0:T(8,128)(2,1)} %shard_map.88), calls=%async_computation.1 | async-start | bytes 1572864 | tf_op jit(solution)/shard_map/all_to_all | solution.py:283
  112.2 14.7 %shard_map.87 = (bf16[8,48,128]{2,1,0:T(8,128)(2,1)}, bf16[8,48,128]{2,1,0:T(8,128)(2,1)}, bf16[8,48,128]{2,1,0:T(8,128)(2,1)}, bf16[8,48,128]{2,1,0:T(8,128)(2,1)}, f32[2]{0:T(128)}) custom-call(s32[1]{0:T(128)} %bitcast.place, bf16[32,480,128]{2,1,0:T(8,128)(2,1)} %all-to-all-done.refs_0_), custom_call_target="tpu_custom_call" | custom-call | tf_op jit(solution)/shard_map/pallas_call | solution.py:170
  127.0 2.4 %collective-permute-start = (bf16[8,48,128]{2,1,0:T(8,128)(2,1)}, bf16[8,48,128]{2,1,0:T(8,128)(2,1)S(1)}, u32[]{:S(2)}, u32[]{:S(2)}) collective-permute-start(bf16[8,48,128]{2,1,0:T(8,128)(2,1)} %get-tuple-element.24), channel_id=1, source_target_pairs={{0,2},{2,0},{4,6},{6,4},{1,3},{3,1},{5,7},{7,5},{8,10},{10,8},{12,... | collective-permute-start | bytes 294920 | tf_op jit(solution)/shard_map/ppermute | solution.py:288
  129.3 3.3 %collective-permute-start.1 = (bf16[8,48,128]{2,1,0:T(8,128)(2,1)}, bf16[8,48,128]{2,1,0:T(8,128)(2,1)S(1)}, u32[]{:S(2)}, u32[]{:S(2)}) collective-permute-start(bf16[8,48,128]{2,1,0:T(8,128)(2,1)} %get-tuple-element.25), channel_id=1, source_target_pairs={{0,4},{2,6},{4,0},{6,2},{1,5},{3,7},{5,1},{7,3},{8,12},{10,14},{12... | collective-permute-start | bytes 294920 | tf_op jit(solution)/shard_map/ppermute | solution.py:288
  132.6 0.1 collective-permute-start.2
  132.7 0.7 all-to-all-done.1.refs_1_
  133.4 0.0 copy-start.3
  133.4 19.9 %shard_map.89 = (bf16[8,48,128]{2,1,0:T(8,128)(2,1)}, bf16[8,48,128]{2,1,0:T(8,128)(2,1)}, f32[2]{0:T(128)}) custom-call(s32[1]{0:T(128)} %bitcast.place, bf16[32,480,128]{2,1,0:T(8,128)(2,1)} %all-to-all-done.refs_0_, bf16[32,96,128]{2,1,0:T(8,128)(2,1)S(1)} %all-to-all-done.1.refs_1_, f32[2]{0:T(128)} %get-tuple-element.28.refs_2_), custom_call_target="tpu_custom_call" | custom-call | tf_op jit(solution)/shard_map/pallas_call | solution.py:170
  153.3 0.0 copy-start.4
  153.3 0.0 collective-permute-done.refs_1_
  153.3 0.0 collective-permute-done.1.refs_2_
  153.3 0.0 collective-permute-done.2.refs_3_
  153.4 0.0 copy-done.3
  153.4 0.8 shard_map.91
  154.1 5.1 %all-to-all-start.2 = ((bf16[8,4,48,128]{3,2,1,0:T(8,128)(2,1)}), bf16[8,4,48,128]{3,2,1,0:T(8,128)(2,1)S(1)}, u32[]{:S(2)}, u32[]{:S(2)}) async-start(bf16[8,4,48,128]{3,2,1,0:T(8,128)(2,1)} %shard_map.91), calls=%async_computation.2 | async-start | bytes 786432 | tf_op jit(solution)/shard_map/all_to_all | solution.py:283
  159.2 0.0 copy-done.4
  159.2 0.0 copy-start.2
  159.2 2.1 collective-permute-start.3
  161.3 19.9 %shard_map.90 = (bf16[8,48,128]{2,1,0:T(8,128)(2,1)}, bf16[8,48,128]{2,1,0:T(8,128)(2,1)}, f32[2]{0:T(128)}) custom-call(s32[1]{0:T(128)} %bitcast.place, bf16[32,480,128]{2,1,0:T(8,128)(2,1)} %all-to-all-done.refs_0_, bf16[32,96,128]{2,1,0:T(8,128)(2,1)S(1)} %all-to-all-done.1.refs_1_, f32[2]{0:T(128)} %get-tuple-element.28.refs_2_), custom_call_target="tpu_custom_call" | custom-call | tf_op jit(solution)/shard_map/pallas_call | solution.py:170
  181.1 0.0 copy-start
  181.2 0.0 copy-start.1
  181.2 3.4 %collective-permute-start.4 = (bf16[8,48,128]{2,1,0:T(8,128)(2,1)}, bf16[8,48,128]{2,1,0:T(8,128)(2,1)S(1)}, u32[]{:S(2)}, u32[]{:S(2)}) collective-permute-start(bf16[8,48,128]{2,1,0:T(8,128)(2,1)} %get-tuple-element.33), channel_id=1, source_target_pairs={{0,4},{2,6},{4,0},{6,2},{1,5},{3,7},{5,1},{7,3},{8,12},{10,14},{12... | collective-permute-start | bytes 294920 | tf_op jit(solution)/shard_map/ppermute | solution.py:288
  184.6 0.4 collective-permute-start.5
  184.9 0.0 collective-permute-done.3.refs_1_
  184.9 4.5 %collective-permute-done.4.refs_2_ = bf16[8,48,128]{2,1,0:T(8,128)(2,1)S(1)} collective-permute-done((bf16[8,48,128]{2,1,0:T(8,128)(2,1)}, bf16[8,48,128]{2,1,0:T(8,128)(2,1)S(1)}, u32[]{:S(2)}, u32[]{:S(2)}) %collective-permute-start.4) | collective-permute-done | bytes 98336 | tf_op jit(solution)/shard_map/ppermute | solution.py:288
  189.5 3.0 %collective-permute-done.5.refs_3_ = bf16[8,48,128]{2,1,0:T(8,128)(2,1)S(1)} collective-permute-done((bf16[8,48,128]{2,1,0:T(8,128)(2,1)}, bf16[8,48,128]{2,1,0:T(8,128)(2,1)S(1)}, u32[]{:S(2)}, u32[]{:S(2)}) %collective-permute-start.5) | collective-permute-done | bytes 98336 | tf_op jit(solution)/shard_map/ppermute | solution.py:288
  192.5 0.0 all-to-all-done.2.refs_0_.guided
  192.5 0.0 copy-done.2
  192.5 0.8 shard_map.92
  193.2 5.1 %all-to-all-start.3 = ((bf16[8,4,48,128]{3,2,1,0:T(8,128)(2,1)}), bf16[8,4,48,128]{3,2,1,0:T(8,128)(2,1)S(1)}, u32[]{:S(2)}, u32[]{:S(2)}) async-start(bf16[8,4,48,128]{3,2,1,0:T(8,128)(2,1)} %shard_map.92), calls=%async_computation.3 | async-start | bytes 786432 | tf_op jit(solution)/shard_map/all_to_all | solution.py:283
  199.0 0.0 copy-done
  199.0 0.0 copy-done.1
  199.1 0.3 shard_map.94.refs_2_
  199.4 5.3 %collective-permute-start.6 = (bf16[48,4096]{1,0:T(8,128)(2,1)S(1)}, bf16[48,4096]{1,0:T(8,128)(2,1)S(1)}, u32[]{:S(2)}, u32[]{:S(2)}) collective-permute-start(bf16[48,4096]{1,0:T(8,128)(2,1)S(1)} %shard_map.94.refs_2_), channel_id=1, source_target_pairs={{0,128},{128,0},{1,129},{129,1},{2,130},{130,2},{3,131},{131,3},{4... | collective-permute-start | bytes 1179656 | tf_op jit(solution)/shard_map/ppermute | solution.py:305
  204.6 1.8 all-to-all-done.3.refs_1_.guided
  206.5 0.3 shard_map.95.refs_3_
  206.8 5.3 %collective-permute-start.7 = (bf16[48,4096]{1,0:T(8,128)(2,1)S(1)}, bf16[48,4096]{1,0:T(8,128)(2,1)S(1)}, u32[]{:S(2)}, u32[]{:S(2)}) collective-permute-start(bf16[48,4096]{1,0:T(8,128)(2,1)S(1)} %shard_map.95.refs_3_), channel_id=1, source_target_pairs={{0,128},{128,0},{1,129},{129,1},{2,130},{130,2},{3,131},{131,3},{4... | collective-permute-start | bytes 1179656 | tf_op jit(solution)/shard_map/ppermute | solution.py:305
  212.7 1.4 shard_map.93
  214.1 0.1 collective-permute-done.6.refs_0_
  214.1 8.4 %collective-permute-done.7.refs_1_ = bf16[48,4096]{1,0:T(8,128)(2,1)S(1)} collective-permute-done((bf16[48,4096]{1,0:T(8,128)(2,1)S(1)}, bf16[48,4096]{1,0:T(8,128)(2,1)S(1)}, u32[]{:S(2)}, u32[]{:S(2)}) %collective-permute-start.7) | collective-permute-done | bytes 393248 | tf_op jit(solution)/shard_map/ppermute | solution.py:305
  222.5 1.0 shard_map.96
Async XLA Ops:
  3.9 99.8 %all-to-all-start = ((bf16[32,480,128]{2,1,0:T(8,128)(2,1)}), bf16[32,480,128]{2,1,0:T(8,128)(2,1)}, u32[]{:S(2)}, u32[]{:S(2)}) async-start(bf16[32,480,128]{2,1,0:T(8,128)(2,1)} %shard_map.86), calls=%async_computation | async-start | bytes 7864320 | tf_op jit(solution)/shard_map/all_to_all | solution.py:283
  103.7 29.7 %all-to-all-start.1 = ((bf16[32,96,128]{2,1,0:T(8,128)(2,1)}), bf16[32,96,128]{2,1,0:T(8,128)(2,1)S(1)}, u32[]{:S(2)}, u32[]{:S(2)}) async-start(bf16[32,96,128]{2,1,0:T(8,128)(2,1)} %shard_map.88), calls=%async_computation.1 | async-start | bytes 1572864 | tf_op jit(solution)/shard_map/all_to_all | solution.py:283
  127.0 26.4 %collective-permute-start = (bf16[8,48,128]{2,1,0:T(8,128)(2,1)}, bf16[8,48,128]{2,1,0:T(8,128)(2,1)S(1)}, u32[]{:S(2)}, u32[]{:S(2)}) collective-permute-start(bf16[8,48,128]{2,1,0:T(8,128)(2,1)} %get-tuple-element.24), channel_id=1, source_target_pairs={{0,2},{2,0},{4,6},{6,4},{1,3},{3,1},{5,7},{7,5},{8,10},{10,8},{12,... | collective-permute-start | bytes 294920 | tf_op jit(solution)/shard_map/ppermute | solution.py:288
  129.3 24.0 %collective-permute-start.1 = (bf16[8,48,128]{2,1,0:T(8,128)(2,1)}, bf16[8,48,128]{2,1,0:T(8,128)(2,1)S(1)}, u32[]{:S(2)}, u32[]{:S(2)}) collective-permute-start(bf16[8,48,128]{2,1,0:T(8,128)(2,1)} %get-tuple-element.25), channel_id=1, source_target_pairs={{0,4},{2,6},{4,0},{6,2},{1,5},{3,7},{5,1},{7,3},{8,12},{10,14},{12... | collective-permute-start | bytes 294920 | tf_op jit(solution)/shard_map/ppermute | solution.py:288
  132.6 20.7 %collective-permute-start.2 = (bf16[8,48,128]{2,1,0:T(8,128)(2,1)}, bf16[8,48,128]{2,1,0:T(8,128)(2,1)S(1)}, u32[]{:S(2)}, u32[]{:S(2)}) collective-permute-start(bf16[8,48,128]{2,1,0:T(8,128)(2,1)} %get-tuple-element.26), channel_id=1, source_target_pairs={{0,6},{2,4},{4,2},{6,0},{1,7},{3,5},{5,3},{7,1},{8,14},{10,12},{12... | collective-permute-start | bytes 294920 | tf_op jit(solution)/shard_map/ppermute | solution.py:288
  133.4 19.9 %copy-start.3 = (bf16[8,48,128]{2,1,0:T(8,128)(2,1)S(1)}, bf16[8,48,128]{2,1,0:T(8,128)(2,1)}, u32[]{:S(2)}) copy-start(bf16[8,48,128]{2,1,0:T(8,128)(2,1)} %get-tuple-element.35.refs_0_) | copy-start | bytes 294916
  153.3 5.9 %copy-start.4 = (bf16[8,48,128]{2,1,0:T(8,128)(2,1)S(1)}, bf16[8,48,128]{2,1,0:T(8,128)(2,1)}, u32[]{:S(2)}) copy-start(bf16[8,48,128]{2,1,0:T(8,128)(2,1)} %get-tuple-element.32) | copy-start | bytes 294916
  154.1 38.3 %all-to-all-start.2 = ((bf16[8,4,48,128]{3,2,1,0:T(8,128)(2,1)}), bf16[8,4,48,128]{3,2,1,0:T(8,128)(2,1)S(1)}, u32[]{:S(2)}, u32[]{:S(2)}) async-start(bf16[8,4,48,128]{3,2,1,0:T(8,128)(2,1)} %shard_map.91), calls=%async_computation.2 | async-start | bytes 786432 | tf_op jit(solution)/shard_map/all_to_all | solution.py:283
  159.2 33.3 %copy-start.2 = (bf16[8,48,128]{2,1,0:T(8,128)(2,1)S(1)}, bf16[8,48,128]{2,1,0:T(8,128)(2,1)}, u32[]{:S(2)}) copy-start(bf16[8,48,128]{2,1,0:T(8,128)(2,1)} %get-tuple-element.40.refs_0_) | copy-start | bytes 294916
  159.2 25.7 %collective-permute-start.3 = (bf16[8,48,128]{2,1,0:T(8,128)(2,1)S(1)}, bf16[8,48,128]{2,1,0:T(8,128)(2,1)S(1)}, u32[]{:S(2)}, u32[]{:S(2)}) collective-permute-start(bf16[8,48,128]{2,1,0:T(8,128)(2,1)S(1)} %copy-done.4), channel_id=1, source_target_pairs={{0,2},{2,0},{4,6},{6,4},{1,3},{3,1},{5,7},{7,5},{8,10},{10,8},{12,... | collective-permute-start | bytes 294920 | tf_op jit(solution)/shard_map/ppermute | solution.py:288
  181.1 17.9 %copy-start = (bf16[1,1,96,4096]{3,2,1,0:T(8,128)(2,1)S(1)}, bf16[1,1,96,4096]{3,2,1,0:T(8,128)(2,1)}, u32[]{:S(2)}) copy-start(bf16[1,1,96,4096]{3,2,1,0:T(8,128)(2,1)} %latents.3) | copy-start | bytes 2359300
  181.2 17.9 %copy-start.1 = (bf16[1,4096]{1,0:T(2,128)(2,1)S(1)}, bf16[1,4096]{1,0:T(2,128)(2,1)}, u32[]{:S(2)}) copy-start(bf16[1,4096]{1,0:T(2,128)(2,1)} %gain.3) | copy-start | bytes 24580
  181.2 8.3 %collective-permute-start.4 = (bf16[8,48,128]{2,1,0:T(8,128)(2,1)}, bf16[8,48,128]{2,1,0:T(8,128)(2,1)S(1)}, u32[]{:S(2)}, u32[]{:S(2)}) collective-permute-start(bf16[8,48,128]{2,1,0:T(8,128)(2,1)} %get-tuple-element.33), channel_id=1, source_target_pairs={{0,4},{2,6},{4,0},{6,2},{1,5},{3,7},{5,1},{7,3},{8,12},{10,14},{12... | collective-permute-start | bytes 294920 | tf_op jit(solution)/shard_map/ppermute | solution.py:288
  184.6 7.9 %collective-permute-start.5 = (bf16[8,48,128]{2,1,0:T(8,128)(2,1)}, bf16[8,48,128]{2,1,0:T(8,128)(2,1)S(1)}, u32[]{:S(2)}, u32[]{:S(2)}) collective-permute-start(bf16[8,48,128]{2,1,0:T(8,128)(2,1)} %get-tuple-element.34), channel_id=1, source_target_pairs={{0,6},{2,4},{4,2},{6,0},{1,7},{3,5},{5,3},{7,1},{8,14},{10,12},{12... | collective-permute-start | bytes 294920 | tf_op jit(solution)/shard_map/ppermute | solution.py:288
  193.2 13.2 %all-to-all-start.3 = ((bf16[8,4,48,128]{3,2,1,0:T(8,128)(2,1)}), bf16[8,4,48,128]{3,2,1,0:T(8,128)(2,1)S(1)}, u32[]{:S(2)}, u32[]{:S(2)}) async-start(bf16[8,4,48,128]{3,2,1,0:T(8,128)(2,1)} %shard_map.92), calls=%async_computation.3 | async-start | bytes 786432 | tf_op jit(solution)/shard_map/all_to_all | solution.py:283
  199.4 14.8 %collective-permute-start.6 = (bf16[48,4096]{1,0:T(8,128)(2,1)S(1)}, bf16[48,4096]{1,0:T(8,128)(2,1)S(1)}, u32[]{:S(2)}, u32[]{:S(2)}) collective-permute-start(bf16[48,4096]{1,0:T(8,128)(2,1)S(1)} %shard_map.94.refs_2_), channel_id=1, source_target_pairs={{0,128},{128,0},{1,129},{129,1},{2,130},{130,2},{3,131},{131,3},{4... | collective-permute-start | bytes 1179656 | tf_op jit(solution)/shard_map/ppermute | solution.py:305
  206.8 15.8 %collective-permute-start.7 = (bf16[48,4096]{1,0:T(8,128)(2,1)S(1)}, bf16[48,4096]{1,0:T(8,128)(2,1)S(1)}, u32[]{:S(2)}, u32[]{:S(2)}) collective-permute-start(bf16[48,4096]{1,0:T(8,128)(2,1)S(1)} %shard_map.95.refs_3_), channel_id=1, source_target_pairs={{0,128},{128,0},{1,129},{129,1},{2,130},{130,2},{3,131},{131,3},{4... | collective-permute-start | bytes 1179656 | tf_op jit(solution)/shard_map/ppermute | solution.py:305

commit v3 on v0

--- a/solution.py
+++ b/solution.py
@@ -83,10 +83,10 @@
     )(*(pltpu.with_memory_space_constraint(a, pltpu.HBM) for a in sources))
 
 
-def attend_kernel(place, *refs, arrays, shard, part, first, groups, normed):
+def attend_kernel(place, *refs, arrays, shard, part, first, groups, normed, joined):
     kv_ref, q_ref = refs[0], refs[arrays - 1]
     norms_in = refs[arrays] if normed else None
-    *outs, norms = refs[-FAR - 1 :]
+    *outs, norms = refs[arrays + normed :]
     peers = kv_ref.shape[0]
     rows = groups * NEAR * part
 
@@ -107,7 +107,9 @@
         own = slice(first + c * part, first + (c + 1) * part)
         pieces = []
         for g in range(groups):
-            other = (pl.program_id(0) * groups + g) ^ place[0]
+            other = pl.program_id(0) * groups + g
+            if not joined:
+                other = other ^ place[0]
             for y in range(NEAR // 2):
                 pieces.append(q_ref[pl.ds(y * 2 * FAR + other * 2, 2), own])
         q = jnp.concatenate(pieces, axis=0).reshape(rows, HDIM)
@@ -127,6 +129,9 @@
     def finish(sums, totals):
         cond, uncond = (s / jnp.sum(t, axis=1, keepdims=True) for s, t in zip(sums, totals))
         guided = (uncond + GUIDANCE * (cond - uncond)).astype(BF16).reshape(groups, NEAR, part, HDIM)
+        if joined:
+            outs[0][pl.ds(pl.program_id(0) * groups, groups)] = guided
+            return
         for step in range(FAR // groups):
 
             @pl.when(pl.program_id(0) == step)
@@ -163,9 +168,10 @@
         finish(sums, totals)
 
 
-def attend(place, arrays, shard, part, first, groups, norms=()):
+def attend(place, arrays, shard, part, first, groups, joined, norms=()):
     smem = pl.BlockSpec(memory_space=pltpu.SMEM)
     whole = pl.BlockSpec(memory_space=pltpu.VMEM)
+    shapes = [(FAR, NEAR, part, HDIM)] if joined else [(NEAR, part, HDIM)] * FAR
     *outs, norms = pl.pallas_call(
         functools.partial(
             attend_kernel,
@@ -174,42 +180,47 @@
             part=part,
             first=first,
             groups=groups,
-            normed=bool(norms),
+            normed=len(norms),
+            joined=joined,
         ),
         grid=(FAR // groups,),
         in_specs=[smem] + [whole for _ in arrays] + [smem for _ in norms],
-        out_specs=[whole] * FAR + [smem],
-        out_shape=[jax.ShapeDtypeStruct((NEAR, part, HDIM), BF16)] * FAR + [jax.ShapeDtypeStruct((2,), F32)],
+        out_specs=[whole] * len(shapes) + [smem],
+        out_shape=[jax.ShapeDtypeStruct(a, BF16) for a in shapes] + [jax.ShapeDtypeStruct((2,), F32)],
         compiler_params=pltpu.CompilerParams(vmem_limit_bytes=ATTEND_VMEM),
     )(place, *(in_vmem(a) for a in arrays), *norms)
     return outs, norms
 
 
-def regroup_kernel(*refs):
+def regroup_kernel(place, *refs):
     *sources, out = refs
+    if len(sources) == 1:
+        for z in range(FAR):
+            out[:, z] = sources[0][z]
+        return
     for d, source in enumerate(sources):
-        out[:, d] = source[...]
-
-
-def regroup(pieces):
-    near, part, _ = pieces[0].shape
+        out[:, pl.ds(d ^ place[0], 1)] = source[...][:, None]
+
+
+def regroup(place, pieces):
+    part = pieces[0].shape[-2]
     return pl.pallas_call(
         regroup_kernel,
-        in_specs=[pl.BlockSpec(memory_space=pltpu.VMEM)] * len(pieces),
+        in_specs=[pl.BlockSpec(memory_space=pltpu.SMEM)] + [pl.BlockSpec(memory_space=pltpu.VMEM)] * len(pieces),
         out_specs=pl.BlockSpec(memory_space=pltpu.VMEM),
-        out_shape=jax.ShapeDtypeStruct((near, len(pieces), part, HDIM), BF16),
+        out_shape=jax.ShapeDtypeStruct((NEAR, FAR, part, HDIM), BF16),
         compiler_params=pltpu.CompilerParams(vmem_limit_bytes=VMEM_LIMIT),
-    )(*(in_vmem(p) for p in pieces))
-
-
-def changed_rows(place, guided, latents, gain, change, out, first):
+    )(place, *(in_vmem(p) for p in pieces))
+
+
+def changed_rows(guided, latents, gain, change, out, first):
     near, far, rows, _ = guided.shape
     heads = near * far
 
     def head(h):
         y, rest = divmod(h, 2 * far)
         z, core = divmod(rest, 2)
-        return guided[2 * y + core, z ^ place[0]].astype(F32)
+        return guided[2 * y + core, z].astype(F32)
 
     total = None
     for h in range(heads):
@@ -224,31 +235,31 @@
         out[:, columns] = (current + change * velocity).astype(BF16)
 
 
-def move_kernel(place, steps, guided, latents, gain, out, *, first):
+def move_kernel(steps, guided, latents, gain, out, *, first):
     change = sigma_of(steps[0, 0] + 1) - sigma_of(steps[0, 0])
-    changed_rows(place, guided, latents, gain, change, out, first)
-
-
-def denoise_kernel(place, steps, *refs):
+    changed_rows(guided, latents, gain, change, out, first)
+
+
+def denoise_kernel(steps, *refs):
     *parts, latents, gain, out = refs
     first = 0
     for guided in parts:
         rows = guided.shape[2]
         to = out.at[0, 0, pl.ds(first, rows)]
-        changed_rows(place, guided, latents, gain, -sigma_of(steps[0, 0]), to, first)
+        changed_rows(guided, latents, gain, -sigma_of(steps[0, 0]), to, first)
         first += rows
 
 
-def update(kernel, out_shape, place, steps_table, parts, latents, gain):
+def update(kernel, out_shape, steps_table, parts, latents, gain):
     smem = pl.BlockSpec(memory_space=pltpu.SMEM)
     whole = pl.BlockSpec(memory_space=pltpu.VMEM)
     return pl.pallas_call(
         kernel,
-        in_specs=[smem, smem] + [whole] * (len(parts) + 2),
+        in_specs=[smem] + [whole] * (len(parts) + 2),
         out_specs=whole,
         out_shape=jax.ShapeDtypeStruct(out_shape, BF16),
         compiler_params=pltpu.CompilerParams(vmem_limit_bytes=VMEM_LIMIT),
-    )(place, steps_table, *(in_vmem(a) for a in (*parts, latents, gain)))
+    )(steps_table, *(in_vmem(a) for a in (*parts, latents, gain)))
 
 
 def choose_kernel(flags, *refs):
@@ -282,30 +293,33 @@
     together = lax.optimization_barrier
 
     def along_z(pieces):
-        return [lax.ppermute(p, Z, [(i, i ^ d) for i in range(FAR)]) if d else p for d, p in enumerate(pieces)]
+        out = list(pieces)
+        for d in (2, 1, 3):
+            out[d] = lax.ppermute(pieces[d], Z, [(i, i ^ d) for i in range(FAR)])
+        return out
 
     kvq = exchange(pack((keys, values, queries), ((0, tokens), (0, tokens), (0, head))), SEQ)
     rest, _ = together((pack((queries,), ((head, tail),)), kvq))
     rest = exchange(rest, SEQ)
-    own, norms = attend(place, (kvq,), tokens, head, 4 * tokens, groups=2)
-    own, rest = together((own, rest))
-    near = along_z(own)
-    own, _ = attend(place, (kvq, rest), tokens, tail, 0, groups=4, norms=(norms,))
+    own, norms = attend(place, (kvq,), tokens, head, 4 * tokens, groups=2, joined=True)
+    own, rest = together((own[0], rest))
+    near = exchange(own, Z)
+    own, _ = attend(place, (kvq, rest), tokens, tail, 0, groups=4, joined=False, norms=(norms,))
     near, own = together((near, own))
     far = along_z(own)
-    guided_head = exchange(regroup(near), (Y, CORE))
+    guided_head = exchange(regroup(place, (near,)), (Y, CORE))
     far, guided_head = together((far, guided_head))
-    guided_tail = exchange(regroup(far), (Y, CORE))
+    guided_tail = exchange(regroup(place, far), (Y, CORE))
 
     swap = lambda a: lax.ppermute(a, "expert", [(0, 1), (1, 0)])
     moved, partner = [], []
     for first, guided in ((0, guided_head), (head, guided_tail)):
         shape = (guided.shape[2], width)
         kernel = functools.partial(move_kernel, first=first)
-        moved.append(update(kernel, shape, place, steps_table, (guided,), latents, gain))
+        moved.append(update(kernel, shape, steps_table, (guided,), latents, gain))
         partner.append(swap(moved[-1]))
     parts = (guided_head, guided_tail)
-    denoised = update(denoise_kernel, latents.shape, place, steps_table, parts, latents, gain)
+    denoised = update(denoise_kernel, latents.shape, steps_table, parts, latents, gain)
     return (denoised, choose(flags, partner, moved, latents.shape))
 
 

time: 221 us -> 222 us (level)
    all_to_all x3 -> x4, starting transfers between devices: 26 us -> 33.9 us  [per_device(): lax.all_to_all(a, axes, split_axis=0, concat_axis=0, tiled=True)]
    ppermute x6 -> x3, starting transfers between devices: 11.7 us -> 6.16 us  [along_z(): out[d] = lax.ppermute(pieces[d], Z, [(i, i ^ d) for i in range(FAR)])]
    all_to_all x3 -> x4, waiting for transfers between devices: 91.4 us -> 93.3 us  [per_device(): lax.all_to_all(a, axes, split_axis=0, concat_axis=0, tiled=True)]
    ppermute x6 -> x3, waiting for transfers between devices: 6.08 us -> 4.65 us  [along_z(): out[d] = lax.ppermute(pieces[d], Z, [(i, i ^ d) for i in range(FAR)])]
  transfers between devices with their start and end apart: 11 -> 9, of which waited for: 4 -> 5; matrix products, arithmetic and copies ran while one was open for 0% -> 0% of each run, Pallas kernels for 26% -> 26%
where the time goes in v3:
time: 222 us
  waiting for transfers between devices  103 us (46%)
  Pallas kernels  62.7 us (28%)
  starting transfers between devices  42.3 us (19%)
  blocking collectives  12.5 us (6%)
    all_to_all x4, waiting for transfers between devices, per_device(): lax.all_to_all(a, axes, split_axis=0, concat_axis=0, tiled=True)  93.3 us
    pallas_call x2, Pallas kernels, attend(): pl.pallas_call(functools.partial(attend_kernel, arrays=len(arrays), shard...  53.7 us
    all_to_all x4, starting transfers between devices, per_device(): lax.all_to_all(a, axes, split_axis=0, concat_axis=0, tiled=True)  33.9 us
    all_to_all x1, blocking collectives, per_device(): lax.all_to_all(a, axes, split_axis=0, concat_axis=0, tiled=True)  12.5 us
    ppermute x3, starting transfers between devices, along_z(): out[d] = lax.ppermute(pieces[d], Z, [(i, i ^ d) for i in range(FAR)])  6.16 us
    pallas_call x2, Pallas kernels, pack(): pl.pallas_call(functools.partial(pack_kernel, spans=spans), in_specs=[pl....  5.21 us
    ppermute x2, waiting for transfers between devices, per_device(): swap = lambda a: lax.ppermute(a, 'expert', [(0, 1), (1, 0)])  4.73 us
    ppermute x3, waiting for transfers between devices, along_z(): out[d] = lax.ppermute(pieces[d], Z, [(i, i ^ d) for i in range(FAR)])  4.65 us
  transfers between devices with their start and end apart: 9, of which 5 were waited for; matrix products, arithmetic and copies ran while one was open for 0% of the time, Pallas kernels for 26%

profile of v3, /device:TPU:1, one launch (start us, length us, event | category | flops | bytes accessed | tf_op | source)
XLA Modules:
  0.0 222.3 jit_solution(285910336277199659)
XLA Ops:
  0.6 3.4 %shard_map.86 = bf16[32,512,128]{2,1,0:T(8,128)(2,1)} custom-call(bf16[1,1,2,96,4096]{4,3,2,1,0:T(8,128)(2,1)} %refs_0_.2, bf16[1,1,2,96,4096]{4,3,2,1,0:T(8,128)(2,1)} %refs_1_.1, bf16[1,1,2,96,4096]{4,3,2,1,0:T(8,128)(2,1)} %refs_0_.3), custom_call_target="tpu_custom_call" | custom-call | tf_op jit(solution)/shard_map/pallas_call | solution.py:71
  4.0 12.8 %all-to-all-start = ((bf16[32,512,128]{2,1,0:T(8,128)(2,1)}), bf16[32,512,128]{2,1,0:T(8,128)(2,1)}, u32[]{:S(2)}, u32[]{:S(2)}) async-start(bf16[32,512,128]{2,1,0:T(8,128)(2,1)} %shard_map.86), calls=%async_computation | async-start | bytes 8388608 | tf_op jit(solution)/shard_map/all_to_all | solution.py:292
  16.9 1.8 shard_map.88
  18.7 91.4 %all-to-all-done.refs_0_ = bf16[32,512,128]{2,1,0:T(8,128)(2,1)} async-done(((bf16[32,512,128]{2,1,0:T(8,128)(2,1)}), bf16[32,512,128]{2,1,0:T(8,128)(2,1)}, u32[]{:S(2)}, u32[]{:S(2)}) %all-to-all-start) | async-done | bytes 4194336 | tf_op jit(solution)/shard_map/all_to_all | solution.py:292
  110.1 7.5 %all-to-all-start.1 = ((bf16[32,64,128]{2,1,0:T(8,128)(2,1)}), bf16[32,64,128]{2,1,0:T(8,128)(2,1)S(1)}, u32[]{:S(2)}, u32[]{:S(2)}) async-start(bf16[32,64,128]{2,1,0:T(8,128)(2,1)} %shard_map.88), calls=%async_computation.1 | async-start | bytes 1048576 | tf_op jit(solution)/shard_map/all_to_all | solution.py:292
  117.6 43.6 %shard_map.87 = (bf16[4,8,64,128]{3,2,1,0:T(8,128)(2,1)}, f32[2]{0:T(128)}) custom-call(s32[1]{0:T(128)} %bitcast.place, bf16[32,512,128]{2,1,0:T(8,128)(2,1)} %all-to-all-done.refs_0_), custom_call_target="tpu_custom_call" | custom-call | tf_op jit(solution)/shard_map/pallas_call | solution.py:175
  161.2 0.0 all-to-all-done.1.refs_1_
  161.2 6.6 %all-to-all-start.2 = ((bf16[4,8,64,128]{3,2,1,0:T(8,128)(2,1)}), bf16[4,8,64,128]{3,2,1,0:T(8,128)(2,1)S(1)}, u32[]{:S(2)}, u32[]{:S(2)}) async-start(bf16[4,8,64,128]{3,2,1,0:T(8,128)(2,1)} %get-tuple-element.23), calls=%async_computation.2 | async-start | bytes 1048576 | tf_op jit(solution)/shard_map/all_to_all | solution.py:292
  167.8 10.1 %shard_map.89 = (bf16[8,32,128]{2,1,0:T(8,128)(2,1)}, bf16[8,32,128]{2,1,0:T(8,128)(2,1)}, bf16[8,32,128]{2,1,0:T(8,128)(2,1)}, bf16[8,32,128]{2,1,0:T(8,128)(2,1)}, f32[2]{0:T(128)}) custom-call(s32[1]{0:T(128)} %bitcast.place, bf16[32,512,128]{2,1,0:T(8,128)(2,1)} %all-to-all-done.refs_0_, bf16[32,64,128]{2,1,0:T(8,128)(2,1)S(1)} %all-to-all-done.1.refs_1_, ...), custom_call_target="tpu_custom_call" | custom-call | tf_op jit(solution)/shard_map/pallas_call | solution.py:175
  177.9 0.0 copy-start.5
  177.9 0.0 copy-start.4
  177.9 0.0 copy-start.3
  177.9 0.0 copy-start
  177.9 0.0 copy-start.1
  178.0 1.9 all-to-all-done.2.refs_0_
  179.8 0.8 shard_map.90
  180.7 0.0 copy-start.2
  180.7 7.1 %all-to-all-start.3 = ((bf16[8,4,64,128]{3,2,1,0:T(8,128)(2,1)}), bf16[8,4,64,128]{3,2,1,0:T(8,128)(2,1)S(1)}, u32[]{:S(2)}, u32[]{:S(2)}) async-start(bf16[8,4,64,128]{3,2,1,0:T(8,128)(2,1)} %shard_map.90), calls=%async_computation.3 | async-start | bytes 1048576 | tf_op jit(solution)/shard_map/all_to_all | solution.py:292
  187.7 0.0 copy-done.5
  187.7 2.2 collective-permute-start
  189.9 0.0 copy-done.4
  189.9 4.0 %collective-permute-start.1 = (bf16[8,32,128]{2,1,0:T(8,128)(2,1)S(1)}, bf16[8,32,128]{2,1,0:T(8,128)(2,1)S(1)}, u32[]{:S(2)}, u32[]{:S(2)}) collective-permute-start(bf16[8,32,128]{2,1,0:T(8,128)(2,1)S(1)} %copy-done.4), channel_id=1, source_target_pairs={{0,4},{2,6},{4,0},{6,2},{1,5},{3,7},{5,1},{7,3},{8,12},{10,14},{12... | collective-permute-start | bytes 196616 | tf_op jit(solution)/shard_map/ppermute | solution.py:298
  193.9 0.0 copy-done.3
  193.9 0.0 collective-permute-start.2
  194.5 0.0 collective-permute-done.refs_1_
  194.5 2.5 %collective-permute-done.1.refs_2_ = bf16[8,32,128]{2,1,0:T(8,128)(2,1)S(1)} collective-permute-done((bf16[8,32,128]{2,1,0:T(8,128)(2,1)S(1)}, bf16[8,32,128]{2,1,0:T(8,128)(2,1)S(1)}, u32[]{:S(2)}, u32[]{:S(2)}) %collective-permute-start.1) | collective-permute-done | bytes 65568 | tf_op jit(solution)/shard_map/ppermute | solution.py:298
  197.0 2.2 collective-permute-done.2.refs_3_
  199.2 0.0 all-to-all-done.3.refs_0_.guided
  199.2 0.0 copy-done
  199.2 0.0 copy-done.1
  199.2 0.4 shard_map.93.refs_2_
  199.6 2.1 collective-permute-start.3
  201.7 0.0 copy-done.2
  201.8 12.5 %all_to_all.25.refs_1_.guided = bf16[8,4,32,128]{3,2,1,0:T(8,128)(2,1)S(1)} all-to-all(bf16[8,4,32,128]{3,2,1,0:T(8,128)(2,1)S(1)} %shard_map.91), channel_id=1, replica_groups=mesh['expert'=2,'batch'=4,'seq_y'=4,'seq_z'=4,'seq_core'=2] {'seq_y','se..., dimensions={0} | all-to-all | bytes 524288 | tf_op jit(solution)/shard_map/all_to_all | solution.py:292
  214.2 0.2 shard_map.94.refs_3_
  214.5 0.1 collective-permute-start.4
  215.2 1.4 shard_map.92
  216.6 4.7 %collective-permute-done.4.refs_1_ = bf16[32,4096]{1,0:T(8,128)(2,1)S(1)} collective-permute-done((bf16[32,4096]{1,0:T(8,128)(2,1)S(1)}, bf16[32,4096]{1,0:T(8,128)(2,1)S(1)}, u32[]{:S(2)}, u32[]{:S(2)}) %collective-permute-start.4) | collective-permute-done | bytes 262176 | tf_op jit(solution)/shard_map/ppermute | solution.py:314
  221.3 0.0 collective-permute-done.3.refs_0_
  221.3 1.0 shard_map.95
  (1 shorter events, 0.0 us)
Async XLA Ops:
  4.0 106.0 %all-to-all-start = ((bf16[32,512,128]{2,1,0:T(8,128)(2,1)}), bf16[32,512,128]{2,1,0:T(8,128)(2,1)}, u32[]{:S(2)}, u32[]{:S(2)}) async-start(bf16[32,512,128]{2,1,0:T(8,128)(2,1)} %shard_map.86), calls=%async_computation | async-start | bytes 8388608 | tf_op jit(solution)/shard_map/all_to_all | solution.py:292
  110.1 51.1 %all-to-all-start.1 = ((bf16[32,64,128]{2,1,0:T(8,128)(2,1)}), bf16[32,64,128]{2,1,0:T(8,128)(2,1)S(1)}, u32[]{:S(2)}, u32[]{:S(2)}) async-start(bf16[32,64,128]{2,1,0:T(8,128)(2,1)} %shard_map.88), calls=%async_computation.1 | async-start | bytes 1048576 | tf_op jit(solution)/shard_map/all_to_all | solution.py:292
  161.2 18.6 %all-to-all-start.2 = ((bf16[4,8,64,128]{3,2,1,0:T(8,128)(2,1)}), bf16[4,8,64,128]{3,2,1,0:T(8,128)(2,1)S(1)}, u32[]{:S(2)}, u32[]{:S(2)}) async-start(bf16[4,8,64,128]{3,2,1,0:T(8,128)(2,1)} %get-tuple-element.23), calls=%async_computation.2 | async-start | bytes 1048576 | tf_op jit(solution)/shard_map/all_to_all | solution.py:292
  177.9 9.8 %copy-start.5 = (bf16[8,32,128]{2,1,0:T(8,128)(2,1)S(1)}, bf16[8,32,128]{2,1,0:T(8,128)(2,1)}, u32[]{:S(2)}) copy-start(bf16[8,32,128]{2,1,0:T(8,128)(2,1)} %get-tuple-element.31) | copy-start | bytes 196612
  177.9 12.0 %copy-start.4 = (bf16[8,32,128]{2,1,0:T(8,128)(2,1)S(1)}, bf16[8,32,128]{2,1,0:T(8,128)(2,1)}, u32[]{:S(2)}) copy-start(bf16[8,32,128]{2,1,0:T(8,128)(2,1)} %get-tuple-element.32) | copy-start | bytes 196612
  177.9 16.0 %copy-start.3 = (bf16[8,32,128]{2,1,0:T(8,128)(2,1)S(1)}, bf16[8,32,128]{2,1,0:T(8,128)(2,1)}, u32[]{:S(2)}) copy-start(bf16[8,32,128]{2,1,0:T(8,128)(2,1)} %get-tuple-element.33) | copy-start | bytes 196612
  177.9 21.3 %copy-start = (bf16[1,1,96,4096]{3,2,1,0:T(8,128)(2,1)S(1)}, bf16[1,1,96,4096]{3,2,1,0:T(8,128)(2,1)}, u32[]{:S(2)}) copy-start(bf16[1,1,96,4096]{3,2,1,0:T(8,128)(2,1)} %latents.3) | copy-start | bytes 2359300
  177.9 21.3 %copy-start.1 = (bf16[1,4096]{1,0:T(2,128)(2,1)S(1)}, bf16[1,4096]{1,0:T(2,128)(2,1)}, u32[]{:S(2)}) copy-start(bf16[1,4096]{1,0:T(2,128)(2,1)} %gain.3) | copy-start | bytes 24580
  180.7 21.1 %copy-start.2 = (bf16[8,32,128]{2,1,0:T(8,128)(2,1)S(1)}, bf16[8,32,128]{2,1,0:T(8,128)(2,1)}, u32[]{:S(2)}) copy-start(bf16[8,32,128]{2,1,0:T(8,128)(2,1)} %get-tuple-element.36.refs_0_) | copy-start | bytes 196612
  180.7 18.5 %all-to-all-start.3 = ((bf16[8,4,64,128]{3,2,1,0:T(8,128)(2,1)}), bf16[8,4,64,128]{3,2,1,0:T(8,128)(2,1)S(1)}, u32[]{:S(2)}, u32[]{:S(2)}) async-start(bf16[8,4,64,128]{3,2,1,0:T(8,128)(2,1)} %shard_map.90), calls=%async_computation.3 | async-start | bytes 1048576 | tf_op jit(solution)/shard_map/all_to_all | solution.py:292
  187.7 6.8 %collective-permute-start = (bf16[8,32,128]{2,1,0:T(8,128)(2,1)S(1)}, bf16[8,32,128]{2,1,0:T(8,128)(2,1)S(1)}, u32[]{:S(2)}, u32[]{:S(2)}) collective-permute-start(bf16[8,32,128]{2,1,0:T(8,128)(2,1)S(1)} %copy-done.5), channel_id=1, source_target_pairs={{0,2},{2,0},{4,6},{6,4},{1,3},{3,1},{5,7},{7,5},{8,10},{10,8},{12,... | collective-permute-start | bytes 196616 | tf_op jit(solution)/shard_map/ppermute | solution.py:298
  189.9 7.1 %collective-permute-start.1 = (bf16[8,32,128]{2,1,0:T(8,128)(2,1)S(1)}, bf16[8,32,128]{2,1,0:T(8,128)(2,1)S(1)}, u32[]{:S(2)}, u32[]{:S(2)}) collective-permute-start(bf16[8,32,128]{2,1,0:T(8,128)(2,1)S(1)} %copy-done.4), channel_id=1, source_target_pairs={{0,4},{2,6},{4,0},{6,2},{1,5},{3,7},{5,1},{7,3},{8,12},{10,14},{12... | collective-permute-start | bytes 196616 | tf_op jit(solution)/shard_map/ppermute | solution.py:298
  193.9 5.3 %collective-permute-start.2 = (bf16[8,32,128]{2,1,0:T(8,128)(2,1)S(1)}, bf16[8,32,128]{2,1,0:T(8,128)(2,1)S(1)}, u32[]{:S(2)}, u32[]{:S(2)}) collective-permute-start(bf16[8,32,128]{2,1,0:T(8,128)(2,1)S(1)} %copy-done.3), channel_id=1, source_target_pairs={{0,6},{2,4},{4,2},{6,0},{1,7},{3,5},{5,3},{7,1},{8,14},{10,12},{12... | collective-permute-start | bytes 196616 | tf_op jit(solution)/shard_map/ppermute | solution.py:298
  199.6 21.7 %collective-permute-start.3 = (bf16[64,4096]{1,0:T(8,128)(2,1)S(1)}, bf16[64,4096]{1,0:T(8,128)(2,1)S(1)}, u32[]{:S(2)}, u32[]{:S(2)}) collective-permute-start(bf16[64,4096]{1,0:T(8,128)(2,1)S(1)} %shard_map.93.refs_2_), channel_id=1, source_target_pairs={{0,128},{128,0},{1,129},{129,1},{2,130},{130,2},{3,131},{131,3},{4... | collective-permute-start | bytes 1572872 | tf_op jit(solution)/shard_map/ppermute | solution.py:314
  214.5 6.8 %collective-permute-start.4 = (bf16[32,4096]{1,0:T(8,128)(2,1)S(1)}, bf16[32,4096]{1,0:T(8,128)(2,1)S(1)}, u32[]{:S(2)}, u32[]{:S(2)}) collective-permute-start(bf16[32,4096]{1,0:T(8,128)(2,1)S(1)} %shard_map.94.refs_3_), channel_id=1, source_target_pairs={{0,128},{128,0},{1,129},{129,1},{2,130},{130,2},{3,131},{131,3},{4... | collective-permute-start | bytes 786440 | tf_op jit(solution)/shard_map/ppermute | solution.py:314

commit v4 on v0

--- a/solution.py
+++ b/solution.py
@@ -275,7 +275,7 @@
 
 def per_device(queries, keys, values, latents, gain, steps_table, flags):
     tokens, width = queries.shape[3:]
-    tail = tokens // 3
+    tail = tokens // 2
     head = tokens - tail
     place = lax.axis_index(Z).reshape(1).astype(jnp.int32)
     exchange = lambda a, axes: lax.all_to_all(a, axes, split_axis=0, concat_axis=0, tiled=True)
@@ -290,7 +290,7 @@
     own, norms = attend(place, (kvq,), tokens, head, 4 * tokens, groups=2)
     own, rest = together((own, rest))
     near = along_z(own)
-    own, _ = attend(place, (kvq, rest), tokens, tail, 0, groups=4, norms=(norms,))
+    own, _ = attend(place, (kvq, rest), tokens, tail, 0, groups=2, norms=(norms,))
     near, own = together((near, own))
     far = along_z(own)
     guided_head = exchange(regroup(near), (Y, CORE))

time: 221 us -> 216 us (0.977); the launches traced: 219 us -> 218 us
  blocking collectives: 11.6 us -> 0 us
  waiting for transfers between devices: 102 us -> 109 us
  starting transfers between devices: 40.5 us -> 46.1 us
    all_to_all x1 -> x0, blocking collectives: 11.6 us -> none  [per_device(): lax.all_to_all(a, axes, split_axis=0, concat_axis=0, tiled=True)]
    all_to_all x3 -> x4, starting transfers between devices: 26 us -> 31.8 us  [per_device(): lax.all_to_all(a, axes, split_axis=0, concat_axis=0, tiled=True)]
    ppermute x2, waiting for transfers between devices: 4.71 us -> 8.41 us  [per_device(): swap = lambda a: lax.ppermute(a, 'expert', [(0, 1), (1, 0)])]
    ppermute x6, waiting for transfers between devices: 6.08 us -> 9.5 us  [along_z(): lax.ppermute(p, Z, [(i, i ^ d) for i in range(FAR)])]
    pallas_call x2, Pallas kernels: 53.9 us -> 51.5 us  [attend(): pl.pallas_call(functools.partial(attend_kernel, arrays=len(arrays), shard...]
    all_to_all x3 -> x4, waiting for transfers between devices: 91.4 us -> 90.7 us  [per_device(): lax.all_to_all(a, axes, split_axis=0, concat_axis=0, tiled=True)]
  transfers between devices with their start and end apart: 11 -> 12, of which waited for: 4 -> 6; matrix products, arithmetic and copies ran while one was open for 0% -> 0% of each run, Pallas kernels for 26% -> 25%
where the time goes in v4:
time: 216 us; the launch traced here: 218 us
  waiting for transfers between devices  109 us (50%)
  Pallas kernels  61.2 us (28%)
  starting transfers between devices  46.1 us (21%)
    all_to_all x4, waiting for transfers between devices, per_device(): lax.all_to_all(a, axes, split_axis=0, concat_axis=0, tiled=True)  90.7 us
    pallas_call x2, Pallas kernels, attend(): pl.pallas_call(functools.partial(attend_kernel, arrays=len(arrays), shard...  51.5 us
    all_to_all x4, starting transfers between devices, per_device(): lax.all_to_all(a, axes, split_axis=0, concat_axis=0, tiled=True)  31.8 us
    ppermute x6, starting transfers between devices, along_z(): lax.ppermute(p, Z, [(i, i ^ d) for i in range(FAR)])  11.4 us
    ppermute x6, waiting for transfers between devices, along_z(): lax.ppermute(p, Z, [(i, i ^ d) for i in range(FAR)])  9.5 us
    ppermute x2, waiting for transfers between devices, per_device(): swap = lambda a: lax.ppermute(a, 'expert', [(0, 1), (1, 0)])  8.41 us
    pallas_call x2, Pallas kernels, pack(): pl.pallas_call(functools.partial(pack_kernel, spans=spans), in_specs=[pl....  5.26 us
  transfers between devices with their start and end apart: 12, of which 6 were waited for; matrix products, arithmetic and copies ran while one was open for 0% of the time, Pallas kernels for 25%

profile of v4, /device:TPU:1, one launch (start us, length us, event | category | flops | bytes accessed | tf_op | source)
XLA Modules:
  0.0 218.0 jit_solution(14124576658617732643)
XLA Ops:
  0.6 3.3 %shard_map.86 = bf16[32,480,128]{2,1,0:T(8,128)(2,1)} custom-call(bf16[1,1,2,96,4096]{4,3,2,1,0:T(8,128)(2,1)} %refs_0_.2, bf16[1,1,2,96,4096]{4,3,2,1,0:T(8,128)(2,1)} %refs_1_.1, bf16[1,1,2,96,4096]{4,3,2,1,0:T(8,128)(2,1)} %refs_0_.3), custom_call_target="tpu_custom_call" | custom-call | tf_op jit(solution)/shard_map/pallas_call | solution.py:71
  3.9 12.8 %all-to-all-start = ((bf16[32,480,128]{2,1,0:T(8,128)(2,1)}), bf16[32,480,128]{2,1,0:T(8,128)(2,1)}, u32[]{:S(2)}, u32[]{:S(2)}) async-start(bf16[32,480,128]{2,1,0:T(8,128)(2,1)} %shard_map.86), calls=%async_computation | async-start | bytes 7864320 | tf_op jit(solution)/shard_map/all_to_all | solution.py:281
  16.7 2.0 shard_map.88
  18.7 85.0 %all-to-all-done.refs_0_ = bf16[32,480,128]{2,1,0:T(8,128)(2,1)} async-done(((bf16[32,480,128]{2,1,0:T(8,128)(2,1)}), bf16[32,480,128]{2,1,0:T(8,128)(2,1)}, u32[]{:S(2)}, u32[]{:S(2)}) %all-to-all-start) | async-done | bytes 3932192 | tf_op jit(solution)/shard_map/all_to_all | solution.py:281
  103.7 8.5 %all-to-all-start.1 = ((bf16[32,96,128]{2,1,0:T(8,128)(2,1)}), bf16[32,96,128]{2,1,0:T(8,128)(2,1)S(1)}, u32[]{:S(2)}, u32[]{:S(2)}) async-start(bf16[32,96,128]{2,1,0:T(8,128)(2,1)} %shard_map.88), calls=%async_computation.1 | async-start | bytes 1572864 | tf_op jit(solution)/shard_map/all_to_all | solution.py:281
  112.2 37.3 %shard_map.87 = (bf16[8,48,128]{2,1,0:T(8,128)(2,1)}, bf16[8,48,128]{2,1,0:T(8,128)(2,1)}, bf16[8,48,128]{2,1,0:T(8,128)(2,1)}, bf16[8,48,128]{2,1,0:T(8,128)(2,1)}, f32[2]{0:T(128)}) custom-call(s32[1]{0:T(128)} %bitcast.place, bf16[32,480,128]{2,1,0:T(8,128)(2,1)} %all-to-all-done.refs_0_), custom_call_target="tpu_custom_call" | custom-call | tf_op jit(solution)/shard_map/pallas_call | solution.py:169
  149.6 0.0 all-to-all-done.1.refs_1_
  149.6 2.4 %collective-permute-start = (bf16[8,48,128]{2,1,0:T(8,128)(2,1)}, bf16[8,48,128]{2,1,0:T(8,128)(2,1)S(1)}, u32[]{:S(2)}, u32[]{:S(2)}) collective-permute-start(bf16[8,48,128]{2,1,0:T(8,128)(2,1)} %get-tuple-element.36), channel_id=1, source_target_pairs={{0,2},{2,0},{4,6},{6,4},{1,3},{3,1},{5,7},{7,5},{8,10},{10,8},{12,... | collective-permute-start | bytes 294920 | tf_op jit(solution)/shard_map/ppermute | solution.py:285
  151.9 3.3 %collective-permute-start.1 = (bf16[8,48,128]{2,1,0:T(8,128)(2,1)}, bf16[8,48,128]{2,1,0:T(8,128)(2,1)S(1)}, u32[]{:S(2)}, u32[]{:S(2)}) collective-permute-start(bf16[8,48,128]{2,1,0:T(8,128)(2,1)} %get-tuple-element.37), channel_id=1, source_target_pairs={{0,4},{2,6},{4,0},{6,2},{1,5},{3,7},{5,1},{7,3},{8,12},{10,14},{12... | collective-permute-start | bytes 294920 | tf_op jit(solution)/shard_map/ppermute | solution.py:285
  155.2 0.1 collective-permute-start.2
  155.3 0.0 copy-start.3
  155.3 14.1 %shard_map.89 = (bf16[8,48,128]{2,1,0:T(8,128)(2,1)}, bf16[8,48,128]{2,1,0:T(8,128)(2,1)}, bf16[8,48,128]{2,1,0:T(8,128)(2,1)}, bf16[8,48,128]{2,1,0:T(8,128)(2,1)}, f32[2]{0:T(128)}) custom-call(s32[1]{0:T(128)} %bitcast.place, bf16[32,480,128]{2,1,0:T(8,128)(2,1)} %all-to-all-done.refs_0_, bf16[32,96,128]{2,1,0:T(8,128)(2,1)S(1)} %all-to-all-done.1.refs_1_, ...), custom_call_target="tpu_custom_call" | custom-call | tf_op jit(solution)/shard_map/pallas_call | solution.py:169
  169.5 0.0 copy-start.6
  169.5 0.0 copy-start.5
  169.5 0.0 copy-start.4
  169.5 0.0 copy-start.2
  169.5 0.0 collective-permute-done.refs_1_
  169.5 0.0 collective-permute-done.1.refs_2_
  169.5 0.0 collective-permute-done.2.refs_3_
  169.6 0.0 copy-done.3
  169.6 0.0 copy-start
  169.6 0.0 copy-start.1
  169.6 0.8 shard_map.90
  170.4 5.6 %all-to-all-start.2 = ((bf16[8,4,48,128]{3,2,1,0:T(8,128)(2,1)}), bf16[8,4,48,128]{3,2,1,0:T(8,128)(2,1)S(1)}, u32[]{:S(2)}, u32[]{:S(2)}) async-start(bf16[8,4,48,128]{3,2,1,0:T(8,128)(2,1)} %shard_map.90), calls=%async_computation.2 | async-start | bytes 786432 | tf_op jit(solution)/shard_map/all_to_all | solution.py:281
  176.0 0.0 copy-done.6
  176.0 2.1 collective-permute-start.3
  178.1 0.0 copy-done.5
  178.1 3.3 %collective-permute-start.4 = (bf16[8,48,128]{2,1,0:T(8,128)(2,1)S(1)}, bf16[8,48,128]{2,1,0:T(8,128)(2,1)S(1)}, u32[]{:S(2)}, u32[]{:S(2)}) collective-permute-start(bf16[8,48,128]{2,1,0:T(8,128)(2,1)S(1)} %copy-done.5), channel_id=1, source_target_pairs={{0,4},{2,6},{4,0},{6,2},{1,5},{3,7},{5,1},{7,3},{8,12},{10,14},{12... | collective-permute-start | bytes 294920 | tf_op jit(solution)/shard_map/ppermute | solution.py:285
  181.4 0.0 copy-done.4
  181.4 0.2 collective-permute-start.5
  181.7 1.7 collective-permute-done.3.refs_1_
  183.3 2.9 %collective-permute-done.4.refs_2_ = bf16[8,48,128]{2,1,0:T(8,128)(2,1)S(1)} collective-permute-done((bf16[8,48,128]{2,1,0:T(8,128)(2,1)S(1)}, bf16[8,48,128]{2,1,0:T(8,128)(2,1)S(1)}, u32[]{:S(2)}, u32[]{:S(2)}) %collective-permute-start.4) | collective-permute-done | bytes 98336 | tf_op jit(solution)/shard_map/ppermute | solution.py:285
  186.2 4.9 %collective-permute-done.5.refs_3_ = bf16[8,48,128]{2,1,0:T(8,128)(2,1)S(1)} collective-permute-done((bf16[8,48,128]{2,1,0:T(8,128)(2,1)S(1)}, bf16[8,48,128]{2,1,0:T(8,128)(2,1)S(1)}, u32[]{:S(2)}, u32[]{:S(2)}) %collective-permute-start.5) | collective-permute-done | bytes 98336 | tf_op jit(solution)/shard_map/ppermute | solution.py:285
  191.2 0.0 all-to-all-done.2.refs_0_.guided
  191.2 0.0 copy-done.2
  191.2 0.8 shard_map.91
  191.9 4.9 %all-to-all-start.3 = ((bf16[8,4,48,128]{3,2,1,0:T(8,128)(2,1)}), bf16[8,4,48,128]{3,2,1,0:T(8,128)(2,1)S(1)}, u32[]{:S(2)}, u32[]{:S(2)}) async-start(bf16[8,4,48,128]{3,2,1,0:T(8,128)(2,1)} %shard_map.91), calls=%async_computation.3 | async-start | bytes 786432 | tf_op jit(solution)/shard_map/all_to_all | solution.py:281
  197.5 0.0 copy-done
  197.5 0.0 copy-done.1
  197.5 0.3 shard_map.93.refs_2_
  197.8 1.4 collective-permute-start.6
  199.2 5.7 %all-to-all-done.3.refs_1_.guided = bf16[8,4,48,128]{3,2,1,0:T(8,128)(2,1)S(1)} async-done(((bf16[8,4,48,128]{3,2,1,0:T(8,128)(2,1)}), bf16[8,4,48,128]{3,2,1,0:T(8,128)(2,1)S(1)}, u32[]{:S(2)}, u32[]{:S(2)}) %all-to-all-start.3) | async-done | bytes 393248 | tf_op jit(solution)/shard_map/all_to_all | solution.py:281
  204.9 0.3 shard_map.94.refs_3_
  205.2 1.4 collective-permute-start.7
  207.3 1.4 shard_map.92
  208.7 0.0 collective-permute-done.6.refs_0_
  208.7 8.4 %collective-permute-done.7.refs_1_ = bf16[48,4096]{1,0:T(8,128)(2,1)S(1)} collective-permute-done((bf16[48,4096]{1,0:T(8,128)(2,1)S(1)}, bf16[48,4096]{1,0:T(8,128)(2,1)S(1)}, u32[]{:S(2)}, u32[]{:S(2)}) %collective-permute-start.7) | collective-permute-done | bytes 393248 | tf_op jit(solution)/shard_map/ppermute | solution.py:300
  217.1 1.0 shard_map.95
Async XLA Ops:
  3.9 99.8 %all-to-all-start = ((bf16[32,480,128]{2,1,0:T(8,128)(2,1)}), bf16[32,480,128]{2,1,0:T(8,128)(2,1)}, u32[]{:S(2)}, u32[]{:S(2)}) async-start(bf16[32,480,128]{2,1,0:T(8,128)(2,1)} %shard_map.86), calls=%async_computation | async-start | bytes 7864320 | tf_op jit(solution)/shard_map/all_to_all | solution.py:281
  103.7 45.9 %all-to-all-start.1 = ((bf16[32,96,128]{2,1,0:T(8,128)(2,1)}), bf16[32,96,128]{2,1,0:T(8,128)(2,1)S(1)}, u32[]{:S(2)}, u32[]{:S(2)}) async-start(bf16[32,96,128]{2,1,0:T(8,128)(2,1)} %shard_map.88), calls=%async_computation.1 | async-start | bytes 1572864 | tf_op jit(solution)/shard_map/all_to_all | solution.py:281
  149.6 19.9 %collective-permute-start = (bf16[8,48,128]{2,1,0:T(8,128)(2,1)}, bf16[8,48,128]{2,1,0:T(8,128)(2,1)S(1)}, u32[]{:S(2)}, u32[]{:S(2)}) collective-permute-start(bf16[8,48,128]{2,1,0:T(8,128)(2,1)} %get-tuple-element.36), channel_id=1, source_target_pairs={{0,2},{2,0},{4,6},{6,4},{1,3},{3,1},{5,7},{7,5},{8,10},{10,8},{12,... | collective-permute-start | bytes 294920 | tf_op jit(solution)/shard_map/ppermute | solution.py:285
  151.9 17.6 %collective-permute-start.1 = (bf16[8,48,128]{2,1,0:T(8,128)(2,1)}, bf16[8,48,128]{2,1,0:T(8,128)(2,1)S(1)}, u32[]{:S(2)}, u32[]{:S(2)}) collective-permute-start(bf16[8,48,128]{2,1,0:T(8,128)(2,1)} %get-tuple-element.37), channel_id=1, source_target_pairs={{0,4},{2,6},{4,0},{6,2},{1,5},{3,7},{5,1},{7,3},{8,12},{10,14},{12... | collective-permute-start | bytes 294920 | tf_op jit(solution)/shard_map/ppermute | solution.py:285
  155.2 14.3 %collective-permute-start.2 = (bf16[8,48,128]{2,1,0:T(8,128)(2,1)}, bf16[8,48,128]{2,1,0:T(8,128)(2,1)S(1)}, u32[]{:S(2)}, u32[]{:S(2)}) collective-permute-start(bf16[8,48,128]{2,1,0:T(8,128)(2,1)} %get-tuple-element.38), channel_id=1, source_target_pairs={{0,6},{2,4},{4,2},{6,0},{1,7},{3,5},{5,3},{7,1},{8,14},{10,12},{12... | collective-permute-start | bytes 294920 | tf_op jit(solution)/shard_map/ppermute | solution.py:285
  155.3 14.2 %copy-start.3 = (bf16[8,48,128]{2,1,0:T(8,128)(2,1)S(1)}, bf16[8,48,128]{2,1,0:T(8,128)(2,1)}, u32[]{:S(2)}) copy-start(bf16[8,48,128]{2,1,0:T(8,128)(2,1)} %get-tuple-element.49.refs_0_) | copy-start | bytes 294916
  169.5 6.5 %copy-start.6 = (bf16[8,48,128]{2,1,0:T(8,128)(2,1)S(1)}, bf16[8,48,128]{2,1,0:T(8,128)(2,1)}, u32[]{:S(2)}) copy-start(bf16[8,48,128]{2,1,0:T(8,128)(2,1)} %get-tuple-element.46) | copy-start | bytes 294916
  169.5 8.6 %copy-start.5 = (bf16[8,48,128]{2,1,0:T(8,128)(2,1)S(1)}, bf16[8,48,128]{2,1,0:T(8,128)(2,1)}, u32[]{:S(2)}) copy-start(bf16[8,48,128]{2,1,0:T(8,128)(2,1)} %get-tuple-element.47) | copy-start | bytes 294916
  169.5 11.9 %copy-start.4 = (bf16[8,48,128]{2,1,0:T(8,128)(2,1)S(1)}, bf16[8,48,128]{2,1,0:T(8,128)(2,1)}, u32[]{:S(2)}) copy-start(bf16[8,48,128]{2,1,0:T(8,128)(2,1)} %get-tuple-element.48) | copy-start | bytes 294916
  169.5 21.6 %copy-start.2 = (bf16[8,48,128]{2,1,0:T(8,128)(2,1)S(1)}, bf16[8,48,128]{2,1,0:T(8,128)(2,1)}, u32[]{:S(2)}) copy-start(bf16[8,48,128]{2,1,0:T(8,128)(2,1)} %get-tuple-element.54.refs_0_) | copy-start | bytes 294916
  169.6 27.9 %copy-start = (bf16[1,1,96,4096]{3,2,1,0:T(8,128)(2,1)S(1)}, bf16[1,1,96,4096]{3,2,1,0:T(8,128)(2,1)}, u32[]{:S(2)}) copy-start(bf16[1,1,96,4096]{3,2,1,0:T(8,128)(2,1)} %latents.3) | copy-start | bytes 2359300
  169.6 27.9 %copy-start.1 = (bf16[1,4096]{1,0:T(2,128)(2,1)S(1)}, bf16[1,4096]{1,0:T(2,128)(2,1)}, u32[]{:S(2)}) copy-start(bf16[1,4096]{1,0:T(2,128)(2,1)} %gain.3) | copy-start | bytes 24580
  170.4 20.8 %all-to-all-start.2 = ((bf16[8,4,48,128]{3,2,1,0:T(8,128)(2,1)}), bf16[8,4,48,128]{3,2,1,0:T(8,128)(2,1)S(1)}, u32[]{:S(2)}, u32[]{:S(2)}) async-start(bf16[8,4,48,128]{3,2,1,0:T(8,128)(2,1)} %shard_map.90), calls=%async_computation.2 | async-start | bytes 786432 | tf_op jit(solution)/shard_map/all_to_all | solution.py:281
  176.0 7.4 %collective-permute-start.3 = (bf16[8,48,128]{2,1,0:T(8,128)(2,1)S(1)}, bf16[8,48,128]{2,1,0:T(8,128)(2,1)S(1)}, u32[]{:S(2)}, u32[]{:S(2)}) collective-permute-start(bf16[8,48,128]{2,1,0:T(8,128)(2,1)S(1)} %copy-done.6), channel_id=1, source_target_pairs={{0,2},{2,0},{4,6},{6,4},{1,3},{3,1},{5,7},{7,5},{8,10},{10,8},{12,... | collective-permute-start | bytes 294920 | tf_op jit(solution)/shard_map/ppermute | solution.py:285
  178.1 8.1 %collective-permute-start.4 = (bf16[8,48,128]{2,1,0:T(8,128)(2,1)S(1)}, bf16[8,48,128]{2,1,0:T(8,128)(2,1)S(1)}, u32[]{:S(2)}, u32[]{:S(2)}) collective-permute-start(bf16[8,48,128]{2,1,0:T(8,128)(2,1)S(1)} %copy-done.5), channel_id=1, source_target_pairs={{0,4},{2,6},{4,0},{6,2},{1,5},{3,7},{5,1},{7,3},{8,12},{10,14},{12... | collective-permute-start | bytes 294920 | tf_op jit(solution)/shard_map/ppermute | solution.py:285
  181.4 9.7 %collective-permute-start.5 = (bf16[8,48,128]{2,1,0:T(8,128)(2,1)S(1)}, bf16[8,48,128]{2,1,0:T(8,128)(2,1)S(1)}, u32[]{:S(2)}, u32[]{:S(2)}) collective-permute-start(bf16[8,48,128]{2,1,0:T(8,128)(2,1)S(1)} %copy-done.4), channel_id=1, source_target_pairs={{0,6},{2,4},{4,2},{6,0},{1,7},{3,5},{5,3},{7,1},{8,14},{10,12},{12... | collective-permute-start | bytes 294920 | tf_op jit(solution)/shard_map/ppermute | solution.py:285
  191.9 13.0 %all-to-all-start.3 = ((bf16[8,4,48,128]{3,2,1,0:T(8,128)(2,1)}), bf16[8,4,48,128]{3,2,1,0:T(8,128)(2,1)S(1)}, u32[]{:S(2)}, u32[]{:S(2)}) async-start(bf16[8,4,48,128]{3,2,1,0:T(8,128)(2,1)} %shard_map.91), calls=%async_computation.3 | async-start | bytes 786432 | tf_op jit(solution)/shard_map/all_to_all | solution.py:281
  197.8 10.9 %collective-permute-start.6 = (bf16[48,4096]{1,0:T(8,128)(2,1)S(1)}, bf16[48,4096]{1,0:T(8,128)(2,1)S(1)}, u32[]{:S(2)}, u32[]{:S(2)}) collective-permute-start(bf16[48,4096]{1,0:T(8,128)(2,1)S(1)} %shard_map.93.refs_2_), channel_id=1, source_target_pairs={{0,128},{128,0},{1,129},{129,1},{2,130},{130,2},{3,131},{131,3},{4... | collective-permute-start | bytes 1179656 | tf_op jit(solution)/shard_map/ppermute | solution.py:300
  205.2 11.9 %collective-permute-start.7 = (bf16[48,4096]{1,0:T(8,128)(2,1)S(1)}, bf16[48,4096]{1,0:T(8,128)(2,1)S(1)}, u32[]{:S(2)}, u32[]{:S(2)}) collective-permute-start(bf16[48,4096]{1,0:T(8,128)(2,1)S(1)} %shard_map.94.refs_3_), channel_id=1, source_target_pairs={{0,128},{128,0},{1,129},{129,1},{2,130},{130,2},{3,131},{131,3},{4... | collective-permute-start | bytes 1179656 | tf_op jit(solution)/shard_map/ppermute | solution.py:300
